TPU v7x, 32 devices: a whole 2x2x4 slice. The times are simulated.
32 devices in a mesh: grp: 2 (over y), seq: 4 (over z), fsdp: 2 (over x), head: 2 (over core).
Axes of the slice: x: 2, y: 2, z: 4, core: 2. Of those that a mesh axis runs over, the one named last changes fastest.
Arguments:
- tokens: bfloat16 [6144, 3072], P(('grp', 'seq'), 'head'), parts along dimension 0
- qkv_weight: bfloat16 [3072, 1536], P('fsdp', 'head'), may hold values from -0.109375 to 0.109375
- shift_mod: float32 [6144], P('grp'), parts along dimension 0, may hold values from -3 to 3
- scale_mod: float32 [6144], P('grp'), parts along dimension 0, may hold values from -2 to 2
- q_gain: float32 [4, 128], P(('fsdp', 'head'))
- k_gain: float32 [4, 128], P(('fsdp', 'head'))
- cached: bfloat16 [6144, 512], P(('grp', 'seq'), ('fsdp', 'head')), parts along dimension 0, may hold values from -6 to 6
- active: int32 [48], P(('grp', 'seq')), parts along dimension 0, may hold values from -1 to 5, as said below
- cache_slot: int32 [48], P(('grp', 'seq')), parts along dimension 0, may hold values from 0 to 5, as said below
Outputs:
- blended: bfloat16 [6144, 512], P(('grp', 'seq'), ('fsdp', 'head')), parts along dimension 0
There are 2 independent parts, one for each index of `grp`. A program takes and returns all parts, laid end to end along the dimension named above; an argument that names none is the same for every part. Nothing has to cross between parts.
Inputs may be any that keep to these rules, and one draw needn't show every extreme that they name: Entries s * 6 to s * 6 + 5 list the active local blocks of index s of seq in rising order, each at most once, followed by -1 for the rest. Over the whole sequence exactly 12 blocks are active; some index of seq has all 6 blocks active and some has none. `cache_slot`: entries s * 6 to s * 6 + 5 are a permutation of 0 to 5.
All inputs are finite; a program needn't handle non-finite values.
Results may differ from a plain program's by a relative error of at most 0.012.
The roundings to bfloat16 on the way count: a program that leaves them out, or rounds other values in their place, can miss the bound.
Values may be sent and summed in bfloat16 or wider, within the bound.
No kernel may reach another device: no remote copies, remote signals or barrier semaphores. Data moves between devices by JAX's collectives and lax.ppermute only.
A program may use at most 64 MiB of HBM per device.

v0:
```python
import functools

import jax
import jax.numpy as jnp
from jax import lax
from jax.experimental import pallas as pl
from jax.experimental.pallas import tpu as pltpu
from jax.sharding import PartitionSpec as P


eps_norm = 1e-06
VMEM = pl.BlockSpec(memory_space=pltpu.VMEM)
SMEM = pl.BlockSpec(memory_space=pltpu.SMEM)
ANY = pl.BlockSpec(memory_space=pl.ANY)


def rms_scaled(vector, gain_row):
    return (
        vector * lax.rsqrt(jnp.mean(vector * vector, axis=-1, keepdims=True) + eps_norm) * gain_row
    )


def call(body, out, ins, flops, scalars=0, scratch=(), limit=16 << 20):
    nbytes = sum(x.size * x.dtype.itemsize for x in ins)
    many = isinstance(out, tuple)
    return pl.pallas_call(
        body,
        out_shape=out,
        in_specs=[SMEM] * scalars + [VMEM] * (len(ins) - scalars),
        out_specs=(VMEM,) * len(out) if many else VMEM,
        scratch_shapes=scratch,
        compiler_params=pltpu.CompilerParams(vmem_limit_bytes=limit),
        cost_estimate=pl.CostEstimate(flops=flops, bytes_accessed=nbytes, transcendentals=0),
    )(*ins)


def shape(dims, dtype):
    return jax.ShapeDtypeStruct(dims, dtype)


def tile_rows(index, tile):
    return pl.ds(pl.multiple_of(index * tile, tile), tile)


def half_moments(values):
    mean = jnp.mean(values, axis=1, keepdims=True)
    centred = values - mean
    return mean, jnp.sum(centred * centred, axis=1, keepdims=True)


def moments_kernel(own_ref, out_ref):
    mean, square = half_moments(own_ref[...].astype(jnp.float32))
    out_ref[...] = jnp.concatenate([mean, square], axis=1)


def moments(own):
    rows, half = own.shape
    tile = rows // 6
    return pl.pallas_call(
        moments_kernel,
        out_shape=shape((rows, 2), jnp.float32),
        grid=(rows // tile,),
        in_specs=[pl.BlockSpec((tile, half), lambda at: (at, 0))],
        out_specs=pl.BlockSpec((tile, 2), lambda at: (at, 0)),
        compiler_params=pltpu.CompilerParams(vmem_limit_bytes=8 << 20),
        cost_estimate=pl.CostEstimate(
            flops=5 * rows * half, bytes_accessed=2 * rows * half, transcendentals=0
        ),
        name="moments",
    )(own)


def columns_of(block, head_dim, parts):
    return pl.ds(pl.multiple_of(block * head_dim, head_dim), parts * head_dim)


def normalise_kernel(tile, second, own_ref, other_ref, near_ref, far_ref, weight_ref, scale_ref,
                     shift_ref, *refs):
    half = own_ref.shape[1]
    head_dim = weight_ref.shape[1] // 6
    mine = lax.axis_index("fsdp")
    matched = mine == lax.axis_index("head")
    take_own = jnp.logical_not(matched) if second else matched
    features = pl.ds(pl.multiple_of((1 - mine if second else mine) * half, half), half)
    scale = 1.0 + scale_ref[:, features]
    shift = shift_ref[:, features]
    if second:
        weight = weight_ref[:, columns_of(3 * mine + 1, head_dim, 1)]
    else:
        weight = jnp.concatenate(
            [
                weight_ref[:, columns_of(3 * (1 - mine), head_dim, 1)],
                weight_ref[:, columns_of(3 * (1 - mine) + 2, head_dim, 1)],
            ],
            axis=1,
        )
    for start in range(0, own_ref.shape[0], tile):
        rows = slice(start, start + tile)
        near_mean, far_mean = near_ref[rows, 0:1], far_ref[rows, 0:1]
        mean = 0.5 * (near_mean + far_mean)
        apart = 0.5 * (near_mean - far_mean)
        var = (near_ref[rows, 1:2] + far_ref[rows, 1:2]) / (2 * half) + apart * apart
        factor = lax.rsqrt(var + eps_norm)
        values = jnp.where(take_own, own_ref[rows, :], other_ref[rows, :]).astype(jnp.float32)
        normed = ((values - mean) * factor * scale + shift).astype(jnp.bfloat16)
        if second:
            first_ref, normed_ref, key_ref = refs
            normed_ref[rows, :] = normed
            key_ref[rows, :] = jnp.dot(
                first_ref[rows, :], weight, preferred_element_type=jnp.float32
            )
        else:
            normed_ref, query_ref, value_ref = refs
            normed_ref[rows, :] = normed
            sums = jnp.dot(normed, weight, preferred_element_type=jnp.float32)
            query_ref[rows, :] = sums[:, :head_dim].astype(query_ref.dtype)
            value_ref[rows, :] = sums[:, head_dim:].astype(value_ref.dtype)


def normalise(own, other, near, far, weight, scale, shift, head_dim, first=None):
    rows, half = own.shape
    second = first is not None
    if second:
        outs = (shape((rows, head_dim), jnp.float32),)
    else:
        outs = (shape((rows, head_dim), jnp.bfloat16),) * 2
    operands = (own, other, near, far, weight, scale, shift) + ((first,) if second else ())
    return call(
        functools.partial(normalise_kernel, rows // 3, second),
        (shape((rows, half), jnp.bfloat16), *outs), operands,
        (2 if second else 4) * rows * half * head_dim,
    )


def project_kernel(normed_ref, weight_ref, query_ref, value_ref):
    head_dim = query_ref.shape[1]
    mine = lax.axis_index("fsdp")
    weight = jnp.concatenate(
        [
            weight_ref[:, columns_of(3 * mine, head_dim, 1)],
            weight_ref[:, columns_of(3 * mine + 2, head_dim, 1)],
        ],
        axis=1,
    )
    sums = jnp.dot(normed_ref[...], weight, preferred_element_type=jnp.float32)
    query_ref[...] = sums[:, :head_dim]
    value_ref[...] = sums[:, head_dim:]


def project(normed, weight, head_dim):
    rows, half = normed.shape
    return call(
        project_kernel, (shape((rows, head_dim), jnp.float32),) * 2, (normed, weight),
        4 * rows * half * head_dim,
    )


def foreign_keys_kernel(weight_ref, out_ref, sem_ref):
    head_dim = out_ref.shape[1]
    cols = columns_of(3 * (1 - lax.axis_index("fsdp")) + 1, head_dim, 1)
    copy = pltpu.make_async_copy(weight_ref.at[:, cols], out_ref, sem_ref)
    copy.start()
    copy.wait()


def foreign_keys(weight, head_dim):
    rows = weight.shape[0]
    return pl.pallas_call(
        foreign_keys_kernel,
        out_shape=shape((rows, head_dim), weight.dtype),
        in_specs=[ANY],
        out_specs=VMEM,
        scratch_shapes=[pltpu.SemaphoreType.DMA],
        compiler_params=pltpu.CompilerParams(vmem_limit_bytes=2 << 20),
        cost_estimate=pl.CostEstimate(
            flops=0, bytes_accessed=4 * rows * head_dim, transcendentals=0
        ),
        name="foreign_keys",
    )(pltpu.with_memory_space_constraint(weight, pltpu.HBM))


def keys_kernel(kept_ref, normed_ref, weight_ref, gain_ref, out_ref):
    key = kept_ref[...] + jnp.dot(
        normed_ref[...], weight_ref[...], preferred_element_type=jnp.float32
    )
    out_ref[...] = rms_scaled(key, gain_ref[...]).astype(out_ref.dtype)


def finish_keys(kept, normed, weight, gain):
    rows, head_dim = kept.shape[0], gain.shape[1]
    return call(
        keys_kernel, shape((rows, head_dim), jnp.bfloat16), (kept, normed, weight, gain),
        2 * normed.size * head_dim,
    )


def finish_kernel(part, kept_ref, got_ref, gain_ref, out_ref):
    row = kept_ref[...] + got_ref[...].astype(jnp.float32)
    if part < 2:
        out_ref[...] = rms_scaled(row, gain_ref[...]).astype(out_ref.dtype)
    else:
        out_ref[...] = row.T.astype(out_ref.dtype)


def finish(part, kept, got, gain):
    dims = got.shape if part < 2 else got.shape[::-1]
    return call(
        functools.partial(finish_kernel, part), shape(dims, jnp.bfloat16), (kept, got, gain),
        10 * got.size,
    )


def attend_kernel(blocks, spans, stage, listed, *refs):
    if listed:
        active_ref, refs = refs[0], refs[1:]
    query_ref, refs = refs[0], refs[1:]
    span_refs, refs = refs[: 2 * spans], refs[2 * spans :]
    if stage == "close":
        given, given_mixed, stats_ref, mixed_ref = refs
    else:
        stats_ref, mixed_ref = refs
    head_dim = query_ref.shape[1]
    width = 2 * query_ref.shape[0] // blocks
    factor = head_dim ** (-0.5) * 1.4426950408889634

    def pair(index):
        cols = slice(index * width, (index + 1) * width)
        queries = query_ref[cols, :]
        if stage == "close":
            top, total, mixed = given[0:1, cols], given[1:2, cols], given_mixed[:, cols]
        for at in range(spans):
            key_ref, value_ref = span_refs[2 * at], span_refs[2 * at + 1]
            scores = lax.dot_general(
                key_ref[...], queries, (((1,), (1,)), ((), ())),
                preferred_element_type=jnp.float32,
            )
            best = jnp.max(scores, axis=0, keepdims=True)
            first = at == 0 and stage != "close"
            new_top = best if first else jnp.maximum(top, best)
            weights = jnp.exp2((scores - new_top) * factor)
            added = jnp.sum(weights, axis=0, keepdims=True)
            product = jnp.dot(
                value_ref[...], weights.astype(jnp.bfloat16), preferred_element_type=jnp.float32
            )
            if first:
                total, mixed = added, product
            else:
                shrink = jnp.exp2((top - new_top) * factor)
                total, mixed = total * shrink + added, mixed * shrink + product
            top = new_top
        stats_ref[0:1, cols] = top
        stats_ref[1:2, cols] = total
        mixed_ref[:, cols] = (mixed if stage == "open" else mixed / total).astype(mixed_ref.dtype)

    for index in range(blocks // 2):
        if listed:
            here = [
                (active_ref[at] == 2 * index) | (active_ref[at] == 2 * index + 1)
                for at in range(blocks)
            ]
            pl.when(functools.reduce(jnp.logical_or, here))(functools.partial(pair, index))
        else:
            pair(index)


def attend(blocks, queries, spans, stage, dtype, state=(), active=None):
    rows, head_dim = queries.shape
    listed = () if active is None else (active,)
    flat = [x for span in spans for x in span]
    return call(
        functools.partial(attend_kernel, blocks, len(spans), stage, bool(listed)),
        (shape((8, rows), jnp.float32), shape((head_dim, rows), dtype)),
        (*listed, queries, *flat, *state),
        4 * queries.size * sum(span[0].shape[0] for span in spans),
        scalars=len(listed),
    )


def peek_kernel(blocks, query_ref, key_ref, given_ref, stats_ref, weights_ref):
    head_dim = query_ref.shape[1]
    width = 2 * query_ref.shape[0] // blocks
    factor = head_dim ** (-0.5) * 1.4426950408889634
    for index in range(blocks // 2):
        cols = slice(index * width, (index + 1) * width)
        scores = lax.dot_general(
            key_ref[...], query_ref[cols, :], (((1,), (1,)), ((), ())),
            preferred_element_type=jnp.float32,
        )
        top = given_ref[0:1, cols]
        new_top = jnp.maximum(top, jnp.max(scores, axis=0, keepdims=True))
        weights = jnp.exp2((scores - new_top) * factor)
        shrink = jnp.exp2((top - new_top) * factor)
        stats_ref[0:1, cols] = new_top
        stats_ref[1:2, cols] = given_ref[1:2, cols] * shrink + jnp.sum(
            weights, axis=0, keepdims=True
        )
        stats_ref[2:3, cols] = shrink
        weights_ref[:, cols] = weights.astype(jnp.bfloat16)


def peek(blocks, queries, keys, given):
    return call(
        functools.partial(peek_kernel, blocks),
        (shape(given.shape, jnp.float32), shape((keys.shape[0], queries.shape[0]), jnp.bfloat16)),
        (queries, keys, given), 2 * queries.size * keys.shape[0],
    )


def close_kernel(stats_ref, weights_ref, value_ref, mixed_ref, out_ref):
    product = jnp.dot(value_ref[...], weights_ref[...], preferred_element_type=jnp.float32)
    out_ref[...] = (
        (mixed_ref[...] * stats_ref[2:3, :] + product) / stats_ref[1:2, :]
    ).astype(out_ref.dtype)


def close(stats, weights, values, mixed):
    return call(
        close_kernel, shape(mixed.shape, jnp.bfloat16), (stats, weights, values, mixed),
        2 * values.size * weights.shape[1],
    )


def stale_kernel(blocks, active_ref, slot_ref, cached_ref, out_ref, fresh_ref):
    rows = cached_ref.shape[0] // blocks
    for block in range(blocks):
        here = functools.reduce(
            jnp.logical_or, [active_ref[at] == block for at in range(blocks)]
        )
        place = slice(block * rows, (block + 1) * rows)
        stale = cached_ref[tile_rows(slot_ref[block], rows), :]
        out_ref[place, :] = jnp.where(here, jnp.zeros_like(stale), stale)
        fresh_ref[:, place] = jnp.full((fresh_ref.shape[0], rows), jnp.where(here, 1.0, 0.0))


def stale_rows(active, slots, cached):
    return call(
        functools.partial(stale_kernel, active.shape[0]),
        (shape(cached.shape, cached.dtype), shape((8, cached.shape[0]), jnp.float32)),
        (active, slots, cached), 8 * cached.size, scalars=2,
    )


def blend_kernel(stale_ref, fresh_ref, *refs):
    out_ref = refs[-1]
    factor = out_ref.shape[1] ** (-0.5) * 1.4426950408889634
    stats, mixes = refs[0:-1:2], refs[1:-1:2]
    top = functools.reduce(jnp.maximum, [ref[0:1, :] for ref in stats])
    parts = [ref[1:2, :] * jnp.exp2((ref[0:1, :] - top) * factor) for ref in stats]
    total = functools.reduce(jnp.add, parts)
    mixed = functools.reduce(
        jnp.add, [ref[...].astype(jnp.float32) * (part / total) for ref, part in zip(mixes, parts)]
    )
    mixed = jnp.where(fresh_ref[0:1, :] > 0.5, mixed, 0.0)
    out_ref[...] = mixed.T.astype(out_ref.dtype) + stale_ref[...]


def blend(stale, fresh, shares):
    return call(
        blend_kernel, shape(stale.shape, stale.dtype),
        (stale, fresh, *[x for share in shares for x in share]), 8 * stale.size,
    )


def swapped_plan(tokens, qkv_weight, shift_mod, scale_mod, q_gain, k_gain, cached, active,
                 cache_slot):
    head_dim = q_gain.shape[1]
    blocks = active.shape[0]
    swap = [(0, 1), (1, 0)]
    beside = [(0, 1), (1, 0), (2, 3), (3, 2)]
    across = [(0, 2), (2, 0), (1, 3), (3, 1)]

    other = lax.ppermute(tokens, "head", swap)
    got_columns = lax.ppermute(foreign_keys(qkv_weight, head_dim), "fsdp", swap)
    near = moments(tokens)
    far = lax.ppermute(near, "head", swap)
    common = (
        tokens, other, near, far, qkv_weight,
        scale_mod.reshape(1, -1), shift_mod.reshape(1, -1), head_dim,
    )
    first, part_query, part_value = normalise(*common)
    got_query = lax.ppermute(part_query, "fsdp", swap)
    got_value = lax.ppermute(part_value, "fsdp", swap)
    second, kept_key = normalise(*common, first=first)

    keys = finish_keys(kept_key, second, got_columns, k_gain)
    beside_keys = lax.ppermute(keys, "seq", beside)
    kept_query, kept_value = project(first, qkv_weight, head_dim)
    queries = finish(0, kept_query, got_query, q_gain)
    visitors = lax.ppermute(queries, "seq", across)
    values = finish(2, kept_value, got_value, k_gain)
    beside_values = lax.ppermute(values, "seq", beside)

    stale, fresh = stale_rows(active, cache_slot, cached)
    stats, mixed = attend(blocks, visitors, [(keys, values)], "open", jnp.float32)
    stats, weights = peek(blocks, visitors, beside_keys, stats)
    lent = close(stats, weights, beside_values, mixed)
    returned = (lax.ppermute(stats, "seq", across), lax.ppermute(lent, "seq", across))
    spans = [(keys, values), (beside_keys, beside_values)]
    own = attend(blocks, queries, spans, "whole", jnp.float32, active=active)
    return blend(stale, fresh, [own, returned])


def gathered_plan(tokens, qkv_weight, shift_mod, scale_mod, q_gain, k_gain, cached, active,
                  cache_slot):
    gathered = lax.all_gather(tokens, "head", axis=1, tiled=True).astype(jnp.float32)
    row_mean = jnp.mean(gathered, axis=1, keepdims=True)
    centred = gathered - row_mean
    row_var = jnp.mean(centred * centred, axis=1, keepdims=True)
    normed = (centred * lax.rsqrt(row_var + eps_norm) * (1.0 + scale_mod) + shift_mod).astype(
        jnp.bfloat16
    )
    columns = lax.all_to_all(qkv_weight, "fsdp", split_axis=1, concat_axis=0, tiled=True)
    head_dim = columns.shape[1] // 3
    projected = jnp.dot(normed, columns, preferred_element_type=jnp.float32)
    queries = rms_scaled(projected[:, :head_dim], q_gain).astype(jnp.bfloat16)
    keys = rms_scaled(projected[:, head_dim : 2 * head_dim], k_gain).astype(jnp.bfloat16)
    values = projected[:, 2 * head_dim :].astype(jnp.bfloat16)
    whole_keys = lax.all_gather(keys, "seq", axis=0, tiled=True)
    whole_values = lax.all_gather(values, "seq", axis=0, tiled=True).T
    rows = tokens.shape[0]
    spans = [
        (whole_keys[at : at + rows], whole_values[:, at : at + rows])
        for at in range(0, whole_keys.shape[0], rows)
    ]
    own = attend(active.shape[0], queries, spans, "whole", jnp.float32, active=active)
    return blend(*stale_rows(active, cache_slot, cached), [own])


def solution(mesh):
    sizes = dict(mesh.shape)

    def per_device(*arrays):
        tokens, weight = arrays[:2]
        laid_out = (sizes["fsdp"], sizes["head"], sizes["seq"]) == (2, 2, 4)
        if laid_out and tokens.shape[0] < weight.shape[0]:
            return swapped_plan(*arrays)
        return gathered_plan(*arrays)

    in_specs = (
        P(("grp", "seq"), "head"),
        P("fsdp", "head"),
        P("grp"),
        P("grp"),
        P(("fsdp", "head"), None),
        P(("fsdp", "head"), None),
        P(("grp", "seq"), ("fsdp", "head")),
        P(("grp", "seq")),
        P(("grp", "seq")),
    )
    out_specs = P(("grp", "seq"), ("fsdp", "head"))
    return jax.shard_map(
        per_device, mesh=mesh, in_specs=in_specs, out_specs=out_specs, check_vma=False
    )
```

profile of v0, /device:TPU:0, one launch (start us, length us, event | category | flops | bytes accessed | tf_op | source)
XLA Modules:
  0.0 49.0 jit_solution(10190056006404887016)
XLA Ops:
  0.6 1.3 %foreign_keys.1 = bf16[1536,128]{1,0:T(8,128)(2,1)S(1)} custom-call(bf16[1536,768]{1,0:T(8,128)(2,1)} %weight_ref.7), custom_call_target="tpu_custom_call" | custom-call | bytes 786432 | tf_op jit(solution)/shard_map/foreign_keys/pallas_call | solution.py:168
  1.9 2.4 %collective-permute-start.3 = (bf16[1536,128]{1,0:T(8,128)(2,1)S(1)}, bf16[1536,128]{1,0:T(8,128)(2,1)S(1)}, u32[]{:S(2)}, u32[]{:S(2)}) collective-permute-start(bf16[1536,128]{1,0:T(8,128)(2,1)S(1)} %foreign_keys.1), channel_id=1, source_target_pairs={{0,2},{2,0},{1,3},{3,1},{4,6},{6,4},{5,7},{7,5},{8,10},{10,8},{9,1... | collective-permute-start | bytes 1179656 | tf_op jit(solution)/shard_map/ppermute | solution.py:373
  4.3 1.6 %moments.1.near_ref = f32[768,2]{1,0:T(8,128)S(1)} custom-call(bf16[768,1536]{1,0:T(8,128)(2,1)S(1)} %copy-done.1), custom_call_target="tpu_custom_call" | custom-call | flops 5898240 | bytes 2359296 | tf_op jit(solution)/shard_map/moments/pallas_call | solution.py:59
  6.4 1.3 %collective-permute-done.1.far_ref = f32[768,2]{1,0:T(8,128)S(1)} collective-permute-done((f32[768,2]{1,0:T(8,128)S(1)}, f32[768,2]{1,0:T(8,128)S(1)}, u32[]{:S(2)}, u32[]{:S(2)}) %collective-permute-start.1) | collective-permute-done | bytes 6176 | tf_op jit(solution)/shard_map/ppermute | solution.py:375
  7.8 1.4 %shard_map.92 = (bf16[768,1536]{1,0:T(8,128)(2,1)S(1)}, bf16[768,128]{1,0:T(8,128)(2,1)S(1)}, bf16[768,128]{1,0:T(8,128)(2,1)S(1)}) custom-call(bf16[768,1536]{1,0:T(8,128)(2,1)S(1)} %copy-done.1, bf16[768,1536]{1,0:T(8,128)(2,1)S(1)} %collective-permute-done.other_ref, f32[768,2]{1,0:T(8,128)S(1)} %moments.1.near_ref, ...), custom_call_target="tpu_custom_call" | custom-call | flops 603979776 | bytes 7114752 | tf_op jit(solution)/shard_map/pallas_call | solution.py:26
  9.2 0.7 %collective-permute-start.2 = (bf16[768,128]{1,0:T(8,128)(2,1)S(1)}, bf16[768,128]{1,0:T(8,128)(2,1)S(1)}, u32[]{:S(2)}, u32[]{:S(2)}) collective-permute-start(bf16[768,128]{1,0:T(8,128)(2,1)S(1)} %get-tuple-element.24), channel_id=1, source_target_pairs={{0,2},{2,0},{1,3},{3,1},{4,6},{6,4},{5,7},{7,5},{8,10},{10,8},{9,1... | collective-permute-start | bytes 589832 | tf_op jit(solution)/shard_map/ppermute | solution.py:381
  9.9 1.4 %collective-permute-start.4 = (bf16[768,128]{1,0:T(8,128)(2,1)S(1)}, bf16[768,128]{1,0:T(8,128)(2,1)S(1)}, u32[]{:S(2)}, u32[]{:S(2)}) collective-permute-start(bf16[768,128]{1,0:T(8,128)(2,1)S(1)} %get-tuple-element.28), channel_id=1, source_target_pairs={{0,2},{2,0},{1,3},{3,1},{4,6},{6,4},{5,7},{7,5},{8,10},{10,8},{9,1... | collective-permute-start | bytes 589832 | tf_op jit(solution)/shard_map/ppermute | solution.py:382
  11.3 1.6 %shard_map.95 = (bf16[768,1536]{1,0:T(8,128)(2,1)S(1)}, f32[768,128]{1,0:T(8,128)S(1)}) custom-call(bf16[768,1536]{1,0:T(8,128)(2,1)S(1)} %copy-done.1, bf16[768,1536]{1,0:T(8,128)(2,1)S(1)} %collective-permute-done.other_ref, f32[768,2]{1,0:T(8,128)S(1)} %moments.1.near_ref, f32[768,2]{1,0:T(8,128)S(1)} %collective-permute-done.1.far_ref, ...), custom_call_target="tpu_custom_call" | custom-call | flops 301989888 | bytes 9474048 | tf_op jit(solution)/shard_map/pallas_call | solution.py:26
  12.9 0.8 %shard_map.93 = (f32[768,128]{1,0:T(8,128)S(1)}, f32[768,128]{1,0:T(8,128)S(1)}) custom-call(bf16[768,1536]{1,0:T(8,128)(2,1)S(1)} %get-tuple-element.22.normed_ref.refs_0_, bf16[1536,768]{1,0:T(8,128)(2,1)S(1)} %copy-done), custom_call_target="tpu_custom_call" | custom-call | flops 603979776 | bytes 4718592 | tf_op jit(solution)/shard_map/pallas_call | solution.py:26
  13.7 4.8 %collective-permute-done.2.got_ref = bf16[768,128]{1,0:T(8,128)(2,1)S(1)} collective-permute-done((bf16[768,128]{1,0:T(8,128)(2,1)S(1)}, bf16[768,128]{1,0:T(8,128)(2,1)S(1)}, u32[]{:S(2)}, u32[]{:S(2)}) %collective-permute-start.2) | collective-permute-done | bytes 196640 | tf_op jit(solution)/shard_map/ppermute | solution.py:381
  18.7 3.2 %collective-permute-start.7 = (bf16[768,128]{1,0:T(8,128)(2,1)S(1)}, bf16[768,128]{1,0:T(8,128)(2,1)S(1)}, u32[]{:S(2)}, u32[]{:S(2)}) collective-permute-start(bf16[768,128]{1,0:T(8,128)(2,1)S(1)} %shard_map.94.refs_1_), channel_id=1, source_target_pairs={{0,8},{8,0},{4,12},{12,4},{1,9},{9,1},{5,13},{13,5},{2,10},{10,2},... | collective-permute-start | bytes 589832 | tf_op jit(solution)/shard_map/ppermute | solution.py:389
  21.9 0.9 %shard_map.96.refs_2_.refs_1_ = bf16[768,128]{1,0:T(8,128)(2,1)S(1)} custom-call(f32[768,128]{1,0:T(8,128)S(1)} %get-tuple-element.25.kept_ref, bf16[768,1536]{1,0:T(8,128)(2,1)S(1)} %get-tuple-element.26.normed_ref, bf16[1536,128]{1,0:T(8,128)(2,1)S(1)} %collective-permute-done.3.weight_ref, f32[1,128]{1,0:T(1,128)S(1)} %copy-done.5), custom_call_target="tpu_custom_call" | custom-call | flops 301989888 | bytes 3146240 | tf_op jit(solution)/shard_map/pallas_call | solution.py:26
  22.8 1.6 %collective-permute-start.5 = (bf16[768,128]{1,0:T(8,128)(2,1)S(1)}, bf16[768,128]{1,0:T(8,128)(2,1)S(1)}, u32[]{:S(2)}, u32[]{:S(2)}) collective-permute-start(bf16[768,128]{1,0:T(8,128)(2,1)S(1)} %shard_map.96.refs_2_.refs_1_), channel_id=1, source_target_pairs={{0,4},{4,0},{8,12},{12,8},{1,5},{5,1},{9,13},{13,9},{2,6},{6,2},{1... | collective-permute-start | bytes 589832 | tf_op jit(solution)/shard_map/ppermute | solution.py:386
  25.1 5.8 %collective-permute-done.7.refs_0_.query_ref = bf16[768,128]{1,0:T(8,128)(2,1)S(1)} collective-permute-done((bf16[768,128]{1,0:T(8,128)(2,1)S(1)}, bf16[768,128]{1,0:T(8,128)(2,1)S(1)}, u32[]{:S(2)}, u32[]{:S(2)}) %collective-permute-start.7) | collective-permute-done | bytes 196640 | tf_op jit(solution)/shard_map/ppermute | solution.py:389
  30.9 1.8 %shard_map.99 = (f32[8,768]{1,0:T(8,128)S(1)}, f32[128,768]{1,0:T(8,128)S(1)}) custom-call(bf16[768,128]{1,0:T(8,128)(2,1)S(1)} %collective-permute-done.7.refs_0_.query_ref, bf16[768,128]{1,0:T(8,128)(2,1)S(1)} %shard_map.96.refs_2_.refs_1_, bf16[128,768]{1,0:T(8,128)(2,1)S(1)} %shard_map.97.refs_3_.refs_2_), custom_call_target="tpu_custom_call" | custom-call | flops 301989888 | bytes 589824 | tf_op jit(solution)/shard_map/pallas_call | solution.py:26
  32.7 1.1 %collective-permute-done.5.refs_4_.key_ref = bf16[768,128]{1,0:T(8,128)(2,1)S(1)} collective-permute-done((bf16[768,128]{1,0:T(8,128)(2,1)S(1)}, bf16[768,128]{1,0:T(8,128)(2,1)S(1)}, u32[]{:S(2)}, u32[]{:S(2)}) %collective-permute-start.5) | collective-permute-done | bytes 196640 | tf_op jit(solution)/shard_map/ppermute | solution.py:386
  33.7 1.0 %shard_map.100 = (f32[8,768]{1,0:T(8,128)S(1)}, bf16[768,768]{1,0:T(8,128)(2,1)S(1)}) custom-call(bf16[768,128]{1,0:T(8,128)(2,1)S(1)} %collective-permute-done.7.refs_0_.query_ref, bf16[768,128]{1,0:T(8,128)(2,1)S(1)} %collective-permute-done.5.refs_4_.key_ref, f32[8,768]{1,0:T(8,128)S(1)} %get-tuple-element.31.given_ref), custom_call_target="tpu_custom_call" | custom-call | flops 150994944 | bytes 417792 | tf_op jit(solution)/shard_map/pallas_call | solution.py:26
  34.7 1.6 %collective-permute-done.6.refs_5_.value_ref = bf16[128,768]{1,0:T(8,128)(2,1)S(1)} collective-permute-done((bf16[128,768]{1,0:T(8,128)(2,1)S(1)}, bf16[128,768]{1,0:T(8,128)(2,1)S(1)}, u32[]{:S(2)}, u32[]{:S(2)}) %collective-permute-start.6) | collective-permute-done | bytes 196640 | tf_op jit(solution)/shard_map/ppermute | solution.py:391
  36.6 0.6 %collective-permute-start.9 = (bf16[128,768]{1,0:T(8,128)(2,1)S(1)}, bf16[128,768]{1,0:T(8,128)(2,1)S(1)}, u32[]{:S(2)}, u32[]{:S(2)}) collective-permute-start(bf16[128,768]{1,0:T(8,128)(2,1)S(1)} %shard_map.101), channel_id=1, source_target_pairs={{0,8},{8,0},{4,12},{12,4},{1,9},{9,1},{5,13},{13,5},{2,10},{10,2},... | collective-permute-start | bytes 589832 | tf_op jit(solution)/shard_map/ppermute | solution.py:397
  37.2 0.6 %shard_map.91 = (bf16[768,128]{1,0:T(8,128)(2,1)S(1)}, f32[8,768]{1,0:T(8,128)S(1)}) custom-call(s32[6]{0:T(128)S(1)} %copy-done.7, s32[6]{0:T(128)S(1)} %copy-done.6, bf16[768,128]{1,0:T(8,128)(2,1)S(1)} %copy-done.2), custom_call_target="tpu_custom_call" | custom-call | flops 786432 | bytes 196656 | tf_op jit(solution)/shard_map/pallas_call | solution.py:26
  37.8 2.5 %collective-permute-start.8 = (f32[8,768]{1,0:T(8,128)S(1)}, f32[8,768]{1,0:T(8,128)S(1)}, u32[]{:S(2)}, u32[]{:S(2)}) collective-permute-start(f32[8,768]{1,0:T(8,128)S(1)} %get-tuple-element.32.stats_ref), channel_id=1, source_target_pairs={{0,8},{8,0},{4,12},{12,4},{1,9},{9,1},{5,13},{13,5},{2,10},{10,2},... | collective-permute-start | bytes 73736 | tf_op jit(solution)/shard_map/ppermute | solution.py:397
  40.3 0.6 %shard_map.98 = (f32[8,768]{1,0:T(8,128)S(1)}, f32[128,768]{1,0:T(8,128)S(1)}) custom-call(s32[6]{0:T(128)S(1)} %copy-done.7, bf16[768,128]{1,0:T(8,128)(2,1)S(1)} %shard_map.94.refs_1_, bf16[768,128]{1,0:T(8,128)(2,1)S(1)} %shard_map.96.refs_2_.refs_1_, bf16[128,768]{1,0:T(8,128)(2,1)S(1)} %shard_map.97.refs_3_.refs_2_, ...), custom_call_target="tpu_custom_call" | custom-call | flops 603979776 | bytes 983064 | tf_op jit(solution)/shard_map/pallas_call | solution.py:26
  40.9 7.2 %collective-permute-done.8.refs_2_ = f32[8,768]{1,0:T(8,128)S(1)} collective-permute-done((f32[8,768]{1,0:T(8,128)S(1)}, f32[8,768]{1,0:T(8,128)S(1)}, u32[]{:S(2)}, u32[]{:S(2)}) %collective-permute-start.8) | collective-permute-done | bytes 24608 | tf_op jit(solution)/shard_map/ppermute | solution.py:397
  48.1 0.8 %shard_map.102 = bf16[768,128]{1,0:T(8,128)(2,1)} custom-call(bf16[768,128]{1,0:T(8,128)(2,1)S(1)} %get-tuple-element.20.stale_ref, f32[8,768]{1,0:T(8,128)S(1)} %get-tuple-element.21.fresh_ref, f32[8,768]{1,0:T(8,128)S(1)} %get-tuple-element.29.refs_0_, f32[128,768]{1,0:T(8,128)S(1)} %get-tuple-element.30.refs_1_, ...), custom_call_target="tpu_custom_call" | custom-call | flops 786432 | bytes 860160 | tf_op jit(solution)/shard_map/pallas_call | solution.py:26
  (28 shorter events, 2.3 us)
Async XLA Ops:
  0.0 4.3 %copy-start.1 = (bf16[768,1536]{1,0:T(8,128)(2,1)S(1)}, bf16[768,1536]{1,0:T(8,128)(2,1)}, u32[]{:S(2)}) copy-start(bf16[768,1536]{1,0:T(8,128)(2,1)} %own_ref.5) | copy-start | bytes 7077892
  0.0 7.8 %copy-start = (bf16[1536,768]{1,0:T(8,128)(2,1)S(1)}, bf16[1536,768]{1,0:T(8,128)(2,1)}, u32[]{:S(2)}) copy-start(bf16[1536,768]{1,0:T(8,128)(2,1)} %weight_ref.7) | copy-start | bytes 7077892
  0.0 7.8 %copy-start.3 = (f32[3072]{0:T(1024)S(1)}, f32[3072]{0:T(1024)}, u32[]{:S(2)}) copy-start(f32[3072]{0:T(1024)} %param.12) | copy-start | bytes 36868
  0.0 7.8 %copy-start.4 = (f32[3072]{0:T(1024)S(1)}, f32[3072]{0:T(1024)}, u32[]{:S(2)}) copy-start(f32[3072]{0:T(1024)} %param.11) | copy-start | bytes 36868
  0.0 7.8 %collective-permute-start = (bf16[768,1536]{1,0:T(8,128)(2,1)}, bf16[768,1536]{1,0:T(8,128)(2,1)S(1)}, u32[]{:S(2)}, u32[]{:S(2)}) collective-permute-start(bf16[768,1536]{1,0:T(8,128)(2,1)} %own_ref.5), channel_id=1, source_target_pairs={{0,1},{1,0},{2,3},{3,2},{4,5},{5,4},{6,7},{7,6},{8,9},{9,8},{10,11... | collective-permute-start | bytes 7077896 | tf_op jit(solution)/shard_map/ppermute | solution.py:372
  1.9 20.0 %collective-permute-start.3 = (bf16[1536,128]{1,0:T(8,128)(2,1)S(1)}, bf16[1536,128]{1,0:T(8,128)(2,1)S(1)}, u32[]{:S(2)}, u32[]{:S(2)}) collective-permute-start(bf16[1536,128]{1,0:T(8,128)(2,1)S(1)} %foreign_keys.1), channel_id=1, source_target_pairs={{0,2},{2,0},{1,3},{3,1},{4,6},{6,4},{5,7},{7,5},{8,10},{10,8},{9,1... | collective-permute-start | bytes 1179656 | tf_op jit(solution)/shard_map/ppermute | solution.py:373
  5.9 1.8 %collective-permute-start.1 = (f32[768,2]{1,0:T(8,128)S(1)}, f32[768,2]{1,0:T(8,128)S(1)}, u32[]{:S(2)}, u32[]{:S(2)}) collective-permute-start(f32[768,2]{1,0:T(8,128)S(1)} %moments.1.near_ref), channel_id=1, source_target_pairs={{0,1},{1,0},{2,3},{3,2},{4,5},{5,4},{6,7},{7,6},{8,9},{9,8},{10,11... | collective-permute-start | bytes 18440 | tf_op jit(solution)/shard_map/ppermute | solution.py:375
  9.2 9.3 %collective-permute-start.2 = (bf16[768,128]{1,0:T(8,128)(2,1)S(1)}, bf16[768,128]{1,0:T(8,128)(2,1)S(1)}, u32[]{:S(2)}, u32[]{:S(2)}) collective-permute-start(bf16[768,128]{1,0:T(8,128)(2,1)S(1)} %get-tuple-element.24), channel_id=1, source_target_pairs={{0,2},{2,0},{1,3},{3,1},{4,6},{6,4},{5,7},{7,5},{8,10},{10,8},{9,1... | collective-permute-start | bytes 589832 | tf_op jit(solution)/shard_map/ppermute | solution.py:381
  9.9 14.5 %collective-permute-start.4 = (bf16[768,128]{1,0:T(8,128)(2,1)S(1)}, bf16[768,128]{1,0:T(8,128)(2,1)S(1)}, u32[]{:S(2)}, u32[]{:S(2)}) collective-permute-start(bf16[768,128]{1,0:T(8,128)(2,1)S(1)} %get-tuple-element.28), channel_id=1, source_target_pairs={{0,2},{2,0},{1,3},{3,1},{4,6},{6,4},{5,7},{7,5},{8,10},{10,8},{9,1... | collective-permute-start | bytes 589832 | tf_op jit(solution)/shard_map/ppermute | solution.py:382
  12.9 5.6 %copy-start.8 = (f32[1,128]{1,0:T(1,128)S(1)}, f32[1,128]{1,0:T(1,128)}, u32[]{:S(2)}) copy-start(f32[1,128]{1,0:T(1,128)} %gain_ref.3) | copy-start | bytes 1540
  12.9 9.0 %copy-start.5 = (f32[1,128]{1,0:T(1,128)S(1)}, f32[1,128]{1,0:T(1,128)}, u32[]{:S(2)}) copy-start(f32[1,128]{1,0:T(1,128)} %gain_ref.5) | copy-start | bytes 1540
  18.7 12.2 %collective-permute-start.7 = (bf16[768,128]{1,0:T(8,128)(2,1)S(1)}, bf16[768,128]{1,0:T(8,128)(2,1)S(1)}, u32[]{:S(2)}, u32[]{:S(2)}) collective-permute-start(bf16[768,128]{1,0:T(8,128)(2,1)S(1)} %shard_map.94.refs_1_), channel_id=1, source_target_pairs={{0,8},{8,0},{4,12},{12,4},{1,9},{9,1},{5,13},{13,5},{2,10},{10,2},... | collective-permute-start | bytes 589832 | tf_op jit(solution)/shard_map/ppermute | solution.py:389
  22.7 14.5 %copy-start.2 = (bf16[768,128]{1,0:T(8,128)(2,1)S(1)}, bf16[768,128]{1,0:T(8,128)(2,1)}, u32[]{:S(2)}) copy-start(bf16[768,128]{1,0:T(8,128)(2,1)} %cached_ref.1) | copy-start | bytes 589828
  22.8 14.5 %copy-start.6 = (s32[6]{0:T(128)S(1)}, s32[6]{0:T(128)}, u32[]{:S(2)}) copy-start(s32[6]{0:T(128)} %slot_ref.1) | copy-start | bytes 76
  22.8 14.4 %copy-start.7 = (s32[6]{0:T(128)S(1)}, s32[6]{0:T(128)}, u32[]{:S(2)}) copy-start(s32[6]{0:T(128)} %refs_0_.1) | copy-start | bytes 76
  22.8 10.9 %collective-permute-start.5 = (bf16[768,128]{1,0:T(8,128)(2,1)S(1)}, bf16[768,128]{1,0:T(8,128)(2,1)S(1)}, u32[]{:S(2)}, u32[]{:S(2)}) collective-permute-start(bf16[768,128]{1,0:T(8,128)(2,1)S(1)} %shard_map.96.refs_2_.refs_1_), channel_id=1, source_target_pairs={{0,4},{4,0},{8,12},{12,8},{1,5},{5,1},{9,13},{13,9},{2,6},{6,2},{1... | collective-permute-start | bytes 589832 | tf_op jit(solution)/shard_map/ppermute | solution.py:386
  24.6 11.7 %collective-permute-start.6 = (bf16[128,768]{1,0:T(8,128)(2,1)S(1)}, bf16[128,768]{1,0:T(8,128)(2,1)S(1)}, u32[]{:S(2)}, u32[]{:S(2)}) collective-permute-start(bf16[128,768]{1,0:T(8,128)(2,1)S(1)} %shard_map.97.refs_3_.refs_2_), channel_id=1, source_target_pairs={{0,4},{4,0},{8,12},{12,8},{1,5},{5,1},{9,13},{13,9},{2,6},{6,2},{1... | collective-permute-start | bytes 589832 | tf_op jit(solution)/shard_map/ppermute | solution.py:391
  36.6 11.5 %collective-permute-start.9 = (bf16[128,768]{1,0:T(8,128)(2,1)S(1)}, bf16[128,768]{1,0:T(8,128)(2,1)S(1)}, u32[]{:S(2)}, u32[]{:S(2)}) collective-permute-start(bf16[128,768]{1,0:T(8,128)(2,1)S(1)} %shard_map.101), channel_id=1, source_target_pairs={{0,8},{8,0},{4,12},{12,4},{1,9},{9,1},{5,13},{13,5},{2,10},{10,2},... | collective-permute-start | bytes 589832 | tf_op jit(solution)/shard_map/ppermute | solution.py:397
  37.8 10.3 %collective-permute-start.8 = (f32[8,768]{1,0:T(8,128)S(1)}, f32[8,768]{1,0:T(8,128)S(1)}, u32[]{:S(2)}, u32[]{:S(2)}) collective-permute-start(f32[8,768]{1,0:T(8,128)S(1)} %get-tuple-element.32.stats_ref), channel_id=1, source_target_pairs={{0,8},{8,0},{4,12},{12,4},{1,9},{9,1},{5,13},{13,5},{2,10},{10,2},... | collective-permute-start | bytes 73736 | tf_op jit(solution)/shard_map/ppermute | solution.py:397
where the time goes:
time: 49.1 us; the launch traced here: 49 us
  waiting for transfers between devices  21.8 us (44%)
  starting transfers between devices  14 us (29%)
  Pallas kernels  13 us (26%)
    pallas_call x12, Pallas kernels, call(): pl.pallas_call(body, out_shape=out, in_specs=[SMEM] * scalars + [VMEM] *...  10 us
    ppermute x1, waiting for transfers between devices, swapped_plan(): lax.ppermute(stats, 'seq', across)  7.23 us
    ppermute x1, waiting for transfers between devices, swapped_plan(): visitors = lax.ppermute(queries, 'seq', across)  5.8 us
    ppermute x1, waiting for transfers between devices, swapped_plan(): got_query = lax.ppermute(part_query, 'fsdp', swap)  4.79 us
    ppermute x1, starting transfers between devices, swapped_plan(): visitors = lax.ppermute(queries, 'seq', across)  3.19 us
    ppermute x1, starting transfers between devices, swapped_plan(): lax.ppermute(stats, 'seq', across)  2.47 us
    ppermute x1, starting transfers between devices, swapped_plan(): got_columns = lax.ppermute(foreign_keys(qkv_weight, head_dim), 'fsdp', swap)  2.44 us
    ppermute x1, starting transfers between devices, swapped_plan(): beside_keys = lax.ppermute(keys, 'seq', beside)  1.64 us
  transfers between devices with their start and end apart: 10, of which 6 were waited for; matrix products, arithmetic and copies ran while one was open for 0% of the time, Pallas kernels for 24%

commit v1 on v0

--- a/solution.py
+++ b/solution.py
@@ -194,40 +194,48 @@
     )
 
 
-def finish_kernel(part, kept_ref, got_ref, gain_ref, out_ref):
+def finish_kernel(part, kept_ref, got_ref, gain_ref, out_ref, *half_refs):
     row = kept_ref[...] + got_ref[...].astype(jnp.float32)
-    if part < 2:
-        out_ref[...] = rms_scaled(row, gain_ref[...]).astype(out_ref.dtype)
+    if part == 0:
+        query = rms_scaled(row, gain_ref[...]).astype(out_ref.dtype)
+        out_ref[...] = query
+        start = 0
+        for ref in half_refs:
+            ref[...] = query[start : start + ref.shape[0], :]
+            start += ref.shape[0]
     else:
         out_ref[...] = row.T.astype(out_ref.dtype)
 
 
-def finish(part, kept, got, gain):
-    dims = got.shape if part < 2 else got.shape[::-1]
-    return call(
-        functools.partial(finish_kernel, part), shape(dims, jnp.bfloat16), (kept, got, gain),
-        10 * got.size,
-    )
-
-
-def attend_kernel(blocks, spans, stage, listed, *refs):
+def finish_queries(kept, got, gain):
+    rows, head_dim = got.shape
+    halves = (shape((rows // 2, head_dim), jnp.bfloat16),) * 2
+    return call(
+        functools.partial(finish_kernel, 0), (shape(got.shape, jnp.bfloat16), *halves),
+        (kept, got, gain), 10 * got.size,
+    )
+
+
+def finish_values(kept, got, gain):
+    return call(
+        functools.partial(finish_kernel, 2), shape(got.shape[::-1], jnp.bfloat16),
+        (kept, got, gain), 10 * got.size,
+    )
+
+
+def attend_kernel(groups, spans, divide, listed, *refs):
     if listed:
         active_ref, refs = refs[0], refs[1:]
     query_ref, refs = refs[0], refs[1:]
     span_refs, refs = refs[: 2 * spans], refs[2 * spans :]
-    if stage == "close":
-        given, given_mixed, stats_ref, mixed_ref = refs
-    else:
-        stats_ref, mixed_ref = refs
+    stats_ref, mixed_ref = refs
     head_dim = query_ref.shape[1]
-    width = 2 * query_ref.shape[0] // blocks
+    width = query_ref.shape[0] // groups
     factor = head_dim ** (-0.5) * 1.4426950408889634
 
     def pair(index):
         cols = slice(index * width, (index + 1) * width)
         queries = query_ref[cols, :]
-        if stage == "close":
-            top, total, mixed = given[0:1, cols], given[1:2, cols], given_mixed[:, cols]
         for at in range(spans):
             key_ref, value_ref = span_refs[2 * at], span_refs[2 * at + 1]
             scores = lax.dot_general(
@@ -235,14 +243,13 @@
                 preferred_element_type=jnp.float32,
             )
             best = jnp.max(scores, axis=0, keepdims=True)
-            first = at == 0 and stage != "close"
-            new_top = best if first else jnp.maximum(top, best)
+            new_top = best if at == 0 else jnp.maximum(top, best)
             weights = jnp.exp2((scores - new_top) * factor)
             added = jnp.sum(weights, axis=0, keepdims=True)
             product = jnp.dot(
                 value_ref[...], weights.astype(jnp.bfloat16), preferred_element_type=jnp.float32
             )
-            if first:
+            if at == 0:
                 total, mixed = added, product
             else:
                 shrink = jnp.exp2((top - new_top) * factor)
@@ -250,37 +257,36 @@
             top = new_top
         stats_ref[0:1, cols] = top
         stats_ref[1:2, cols] = total
-        mixed_ref[:, cols] = (mixed if stage == "open" else mixed / total).astype(mixed_ref.dtype)
-
-    for index in range(blocks // 2):
+        mixed_ref[:, cols] = mixed / total if divide else mixed
+
+    for index in range(groups):
         if listed:
-            here = [
-                (active_ref[at] == 2 * index) | (active_ref[at] == 2 * index + 1)
-                for at in range(blocks)
-            ]
+            blocks = active_ref.shape[0]
+            here = [active_ref[at] * groups // blocks == index for at in range(blocks)]
+            here = [hit & (active_ref[at] >= 0) for at, hit in enumerate(here)]
             pl.when(functools.reduce(jnp.logical_or, here))(functools.partial(pair, index))
         else:
             pair(index)
 
 
-def attend(blocks, queries, spans, stage, dtype, state=(), active=None):
+def attend(groups, queries, spans, divide, active=None):
     rows, head_dim = queries.shape
     listed = () if active is None else (active,)
     flat = [x for span in spans for x in span]
     return call(
-        functools.partial(attend_kernel, blocks, len(spans), stage, bool(listed)),
-        (shape((8, rows), jnp.float32), shape((head_dim, rows), dtype)),
-        (*listed, queries, *flat, *state),
+        functools.partial(attend_kernel, groups, len(spans), divide, bool(listed)),
+        (shape((8, rows), jnp.float32), shape((head_dim, rows), jnp.float32)),
+        (*listed, queries, *flat),
         4 * queries.size * sum(span[0].shape[0] for span in spans),
         scalars=len(listed),
     )
 
 
-def peek_kernel(blocks, query_ref, key_ref, given_ref, stats_ref, weights_ref):
+def peek_kernel(groups, query_ref, key_ref, given_ref, stats_ref, weights_ref):
     head_dim = query_ref.shape[1]
-    width = 2 * query_ref.shape[0] // blocks
+    width = query_ref.shape[0] // groups
     factor = head_dim ** (-0.5) * 1.4426950408889634
-    for index in range(blocks // 2):
+    for index in range(groups):
         cols = slice(index * width, (index + 1) * width)
         scores = lax.dot_general(
             key_ref[...], query_ref[cols, :], (((1,), (1,)), ((), ())),
@@ -298,9 +304,9 @@
         weights_ref[:, cols] = weights.astype(jnp.bfloat16)
 
 
-def peek(blocks, queries, keys, given):
-    return call(
-        functools.partial(peek_kernel, blocks),
+def peek(groups, queries, keys, given):
+    return call(
+        functools.partial(peek_kernel, groups),
         (shape(given.shape, jnp.float32), shape((keys.shape[0], queries.shape[0]), jnp.bfloat16)),
         (queries, keys, given), 2 * queries.size * keys.shape[0],
     )
@@ -340,24 +346,31 @@
     )
 
 
-def blend_kernel(stale_ref, fresh_ref, *refs):
+def blend_kernel(pieces, stale_ref, fresh_ref, *refs):
     out_ref = refs[-1]
     factor = out_ref.shape[1] ** (-0.5) * 1.4426950408889634
-    stats, mixes = refs[0:-1:2], refs[1:-1:2]
-    top = functools.reduce(jnp.maximum, [ref[0:1, :] for ref in stats])
-    parts = [ref[1:2, :] * jnp.exp2((ref[0:1, :] - top) * factor) for ref in stats]
+    shares, at = [], 0
+    for count in pieces:
+        taken = refs[at : at + 2 * count]
+        at += 2 * count
+        stats = jnp.concatenate([ref[0:2, :] for ref in taken[0::2]], axis=1)
+        mixed = jnp.concatenate([ref[...] for ref in taken[1::2]], axis=1).astype(jnp.float32)
+        shares.append((stats[0:1, :], stats[1:2, :], mixed))
+    top = functools.reduce(jnp.maximum, [best for best, _, _ in shares])
+    parts = [total * jnp.exp2((best - top) * factor) for best, total, _ in shares]
     total = functools.reduce(jnp.add, parts)
     mixed = functools.reduce(
-        jnp.add, [ref[...].astype(jnp.float32) * (part / total) for ref, part in zip(mixes, parts)]
+        jnp.add, [mixed * (part / total) for (_, _, mixed), part in zip(shares, parts)]
     )
     mixed = jnp.where(fresh_ref[0:1, :] > 0.5, mixed, 0.0)
     out_ref[...] = mixed.T.astype(out_ref.dtype) + stale_ref[...]
 
 
 def blend(stale, fresh, shares):
-    return call(
-        blend_kernel, shape(stale.shape, stale.dtype),
-        (stale, fresh, *[x for share in shares for x in share]), 8 * stale.size,
+    flat = [x for share in shares for piece in share for x in piece]
+    return call(
+        functools.partial(blend_kernel, [len(share) for share in shares]),
+        shape(stale.shape, stale.dtype), (stale, fresh, *flat), 8 * stale.size,
     )
 
 
@@ -385,19 +398,22 @@
     keys = finish_keys(kept_key, second, got_columns, k_gain)
     beside_keys = lax.ppermute(keys, "seq", beside)
     kept_query, kept_value = project(first, qkv_weight, head_dim)
-    queries = finish(0, kept_query, got_query, q_gain)
-    visitors = lax.ppermute(queries, "seq", across)
-    values = finish(2, kept_value, got_value, k_gain)
+    queries, *halves = finish_queries(kept_query, got_query, q_gain)
+    visitors = [lax.ppermute(half, "seq", across) for half in halves]
+    values = finish_values(kept_value, got_value, k_gain)
     beside_values = lax.ppermute(values, "seq", beside)
 
     stale, fresh = stale_rows(active, cache_slot, cached)
-    stats, mixed = attend(blocks, visitors, [(keys, values)], "open", jnp.float32)
-    stats, weights = peek(blocks, visitors, beside_keys, stats)
-    lent = close(stats, weights, beside_values, mixed)
-    returned = (lax.ppermute(stats, "seq", across), lax.ppermute(lent, "seq", across))
+    returned = []
+    for visiting in visitors:
+        stats, mixed = attend(1, visiting, [(keys, values)], False)
+        stats, weights = peek(1, visiting, beside_keys, stats)
+        got_stats = lax.ppermute(stats, "seq", across)
+        lent = close(stats, weights, beside_values, mixed)
+        returned.append((got_stats, lax.ppermute(lent, "seq", across)))
     spans = [(keys, values), (beside_keys, beside_values)]
-    own = attend(blocks, queries, spans, "whole", jnp.float32, active=active)
-    return blend(stale, fresh, [own, returned])
+    own = attend(blocks // 2, queries, spans, True, active=active)
+    return blend(stale, fresh, [[own], returned])
 
 
 def gathered_plan(tokens, qkv_weight, shift_mod, scale_mod, q_gain, k_gain, cached, active,
@@ -422,8 +438,8 @@
         (whole_keys[at : at + rows], whole_values[:, at : at + rows])
         for at in range(0, whole_keys.shape[0], rows)
     ]
-    own = attend(active.shape[0], queries, spans, "whole", jnp.float32, active=active)
-    return blend(*stale_rows(active, cache_slot, cached), [own])
+    own = attend(active.shape[0] // 2, queries, spans, True, active=active)
+    return blend(*stale_rows(active, cache_slot, cached), [[own]])
 
 
 def solution(mesh):

time: 49.1 us -> 50.4 us (1.026)
  starting transfers between devices: 14 us -> 19 us
  waiting for transfers between devices: 21.8 us -> 17.8 us
    ppermute x1, waiting for transfers between devices: 4.79 us -> 1.84 us  [swapped_plan(): got_query = lax.ppermute(part_query, 'fsdp', swap)]
    ppermute x3 -> x6, starting transfers between devices: 6.25 us -> 9.04 us  [the longest x2 3.04 us: swapped_plan(): returned.append((got_stats, lax.ppermute(lent, 'seq', across)))]
    ppermute x1, starting transfers between devices: 0.51 us -> 2.18 us  [swapped_plan(): beside_values = lax.ppermute(values, 'seq', beside)]
    ppermute x1, waiting for transfers between devices: 1.6 us -> 0.01 us  [swapped_plan(): beside_values = lax.ppermute(values, 'seq', beside)]
    ppermute x1, waiting for transfers between devices: 0.01 us -> 1.4 us  [swapped_plan(): got_columns = lax.ppermute(foreign_keys(qkv_weight, head_dim), 'fsdp', swap)]
    ppermute x1, waiting for transfers between devices: 1.06 us -> 0.01 us  [swapped_plan(): beside_keys = lax.ppermute(keys, 'seq', beside)]
    ppermute x1, starting transfers between devices: 0.7 us -> 1.39 us  [swapped_plan(): got_query = lax.ppermute(part_query, 'fsdp', swap)]
    ppermute x1, starting transfers between devices: 1.39 us -> 0.7 us  [swapped_plan(): got_value = lax.ppermute(part_value, 'fsdp', swap)]
  transfers between devices with their start and end apart: 10 -> 13, of which waited for: 6 -> 8; matrix products, arithmetic and copies ran while one was open for 0% -> 0% of each run, Pallas kernels for 24% -> 24%
where the time goes in v1:
time: 50.4 us; the launch traced here: 50.3 us
  starting transfers between devices  19 us (38%)
  waiting for transfers between devices  17.8 us (35%)
  Pallas kernels  13.3 us (26%)
    pallas_call x15, Pallas kernels, call(): pl.pallas_call(body, out_shape=out, in_specs=[SMEM] * scalars + [VMEM] *...  10.3 us
    ppermute x2, waiting for transfers between devices, swapped_plan(): visitors = [lax.ppermute(half, 'seq', across) for half in halves]  7.72 us
    ppermute x2, waiting for transfers between devices, swapped_plan(): got_stats = lax.ppermute(stats, 'seq', across)  5.12 us
    ppermute x2, starting transfers between devices, swapped_plan(): returned.append((got_stats, lax.ppermute(lent, 'seq', across)))  3.04 us
    ppermute x2, starting transfers between devices, swapped_plan(): visitors = [lax.ppermute(half, 'seq', across) for half in halves]  3.01 us
    ppermute x2, starting transfers between devices, swapped_plan(): got_stats = lax.ppermute(stats, 'seq', across)  2.99 us
    ppermute x1, starting transfers between devices, swapped_plan(): got_columns = lax.ppermute(foreign_keys(qkv_weight, head_dim), 'fsdp', swap)  2.44 us
    ppermute x1, starting transfers between devices, swapped_plan(): beside_values = lax.ppermute(values, 'seq', beside)  2.18 us
  transfers between devices with their start and end apart: 13, of which 8 were waited for; matrix products, arithmetic and copies ran while one was open for 0% of the time, Pallas kernels for 24%

profile of v1, /device:TPU:0, one launch (start us, length us, event | category | flops | bytes accessed | tf_op | source)
XLA Modules:
  0.0 50.3 jit_solution(12232137584401299044)
XLA Ops:
  0.6 1.3 %foreign_keys.1 = bf16[1536,128]{1,0:T(8,128)(2,1)S(1)} custom-call(bf16[1536,768]{1,0:T(8,128)(2,1)} %weight_ref.7), custom_call_target="tpu_custom_call" | custom-call | bytes 786432 | tf_op jit(solution)/shard_map/foreign_keys/pallas_call | solution.py:168
  1.9 2.4 %collective-permute-start.3 = (bf16[1536,128]{1,0:T(8,128)(2,1)S(1)}, bf16[1536,128]{1,0:T(8,128)(2,1)S(1)}, u32[]{:S(2)}, u32[]{:S(2)}) collective-permute-start(bf16[1536,128]{1,0:T(8,128)(2,1)S(1)} %foreign_keys.1), channel_id=1, source_target_pairs={{0,2},{2,0},{1,3},{3,1},{4,6},{6,4},{5,7},{7,5},{8,10},{10,8},{9,1... | collective-permute-start | bytes 1179656 | tf_op jit(solution)/shard_map/ppermute | solution.py:386
  4.3 1.6 %moments.1.near_ref = f32[768,2]{1,0:T(8,128)S(1)} custom-call(bf16[768,1536]{1,0:T(8,128)(2,1)S(1)} %copy-done.1), custom_call_target="tpu_custom_call" | custom-call | flops 5898240 | bytes 2359296 | tf_op jit(solution)/shard_map/moments/pallas_call | solution.py:59
  6.4 1.3 %collective-permute-done.1.far_ref = f32[768,2]{1,0:T(8,128)S(1)} collective-permute-done((f32[768,2]{1,0:T(8,128)S(1)}, f32[768,2]{1,0:T(8,128)S(1)}, u32[]{:S(2)}, u32[]{:S(2)}) %collective-permute-start.1) | collective-permute-done | bytes 6176 | tf_op jit(solution)/shard_map/ppermute | solution.py:388
  7.8 1.4 %shard_map.92 = (bf16[768,1536]{1,0:T(8,128)(2,1)S(1)}, bf16[768,128]{1,0:T(8,128)(2,1)S(1)}, bf16[768,128]{1,0:T(8,128)(2,1)S(1)}) custom-call(bf16[768,1536]{1,0:T(8,128)(2,1)S(1)} %copy-done.1, bf16[768,1536]{1,0:T(8,128)(2,1)S(1)} %collective-permute-done.other_ref, f32[768,2]{1,0:T(8,128)S(1)} %moments.1.near_ref, ...), custom_call_target="tpu_custom_call" | custom-call | flops 603979776 | bytes 7114752 | tf_op jit(solution)/shard_map/pallas_call | solution.py:26
  9.2 0.7 %collective-permute-start.4 = (bf16[768,128]{1,0:T(8,128)(2,1)S(1)}, bf16[768,128]{1,0:T(8,128)(2,1)S(1)}, u32[]{:S(2)}, u32[]{:S(2)}) collective-permute-start(bf16[768,128]{1,0:T(8,128)(2,1)S(1)} %get-tuple-element.36), channel_id=1, source_target_pairs={{0,2},{2,0},{1,3},{3,1},{4,6},{6,4},{5,7},{7,5},{8,10},{10,8},{9,1... | collective-permute-start | bytes 589832 | tf_op jit(solution)/shard_map/ppermute | solution.py:395
  9.9 1.4 %collective-permute-start.2 = (bf16[768,128]{1,0:T(8,128)(2,1)S(1)}, bf16[768,128]{1,0:T(8,128)(2,1)S(1)}, u32[]{:S(2)}, u32[]{:S(2)}) collective-permute-start(bf16[768,128]{1,0:T(8,128)(2,1)S(1)} %get-tuple-element.31), channel_id=1, source_target_pairs={{0,2},{2,0},{1,3},{3,1},{4,6},{6,4},{5,7},{7,5},{8,10},{10,8},{9,1... | collective-permute-start | bytes 589832 | tf_op jit(solution)/shard_map/ppermute | solution.py:394
  11.3 1.6 %shard_map.95 = (bf16[768,1536]{1,0:T(8,128)(2,1)S(1)}, f32[768,128]{1,0:T(8,128)S(1)}) custom-call(bf16[768,1536]{1,0:T(8,128)(2,1)S(1)} %copy-done.1, bf16[768,1536]{1,0:T(8,128)(2,1)S(1)} %collective-permute-done.other_ref, f32[768,2]{1,0:T(8,128)S(1)} %moments.1.near_ref, f32[768,2]{1,0:T(8,128)S(1)} %collective-permute-done.1.far_ref, ...), custom_call_target="tpu_custom_call" | custom-call | flops 301989888 | bytes 9474048 | tf_op jit(solution)/shard_map/pallas_call | solution.py:26
  12.9 1.4 %collective-permute-done.3.weight_ref = bf16[1536,128]{1,0:T(8,128)(2,1)S(1)} collective-permute-done((bf16[1536,128]{1,0:T(8,128)(2,1)S(1)}, bf16[1536,128]{1,0:T(8,128)(2,1)S(1)}, u32[]{:S(2)}, u32[]{:S(2)}) %collective-permute-start.3) | collective-permute-done | bytes 393248 | tf_op jit(solution)/shard_map/ppermute | solution.py:386
  14.3 0.9 %shard_map.96.refs_2_.refs_1_ = bf16[768,128]{1,0:T(8,128)(2,1)S(1)} custom-call(f32[768,128]{1,0:T(8,128)S(1)} %get-tuple-element.33.kept_ref, bf16[768,1536]{1,0:T(8,128)(2,1)S(1)} %get-tuple-element.34.normed_ref, bf16[1536,128]{1,0:T(8,128)(2,1)S(1)} %collective-permute-done.3.weight_ref, f32[1,128]{1,0:T(1,128)S(1)} %copy-done.5), custom_call_target="tpu_custom_call" | custom-call | flops 301989888 | bytes 3146240 | tf_op jit(solution)/shard_map/pallas_call | solution.py:26
  15.2 2.2 %collective-permute-start.5 = (bf16[768,128]{1,0:T(8,128)(2,1)S(1)}, bf16[768,128]{1,0:T(8,128)(2,1)S(1)}, u32[]{:S(2)}, u32[]{:S(2)}) collective-permute-start(bf16[768,128]{1,0:T(8,128)(2,1)S(1)} %shard_map.96.refs_2_.refs_1_), channel_id=1, source_target_pairs={{0,4},{4,0},{8,12},{12,8},{1,5},{5,1},{9,13},{13,9},{2,6},{6,2},{1... | collective-permute-start | bytes 589832 | tf_op jit(solution)/shard_map/ppermute | solution.py:399
  17.3 0.8 %shard_map.93 = (f32[768,128]{1,0:T(8,128)S(1)}, f32[768,128]{1,0:T(8,128)S(1)}) custom-call(bf16[768,1536]{1,0:T(8,128)(2,1)S(1)} %get-tuple-element.29.normed_ref.refs_0_, bf16[1536,768]{1,0:T(8,128)(2,1)S(1)} %copy-done), custom_call_target="tpu_custom_call" | custom-call | flops 603979776 | bytes 4718592 | tf_op jit(solution)/shard_map/pallas_call | solution.py:26
  18.7 2.2 %collective-permute-start.6 = (bf16[128,768]{1,0:T(8,128)(2,1)S(1)}, bf16[128,768]{1,0:T(8,128)(2,1)S(1)}, u32[]{:S(2)}, u32[]{:S(2)}) collective-permute-start(bf16[128,768]{1,0:T(8,128)(2,1)S(1)} %shard_map.97.refs_3_.refs_2_), channel_id=1, source_target_pairs={{0,4},{4,0},{8,12},{12,8},{1,5},{5,1},{9,13},{13,9},{2,6},{6,2},{1... | collective-permute-start | bytes 589832 | tf_op jit(solution)/shard_map/ppermute | solution.py:404
  20.8 1.8 %collective-permute-done.2.got_ref = bf16[768,128]{1,0:T(8,128)(2,1)S(1)} collective-permute-done((bf16[768,128]{1,0:T(8,128)(2,1)S(1)}, bf16[768,128]{1,0:T(8,128)(2,1)S(1)}, u32[]{:S(2)}, u32[]{:S(2)}) %collective-permute-start.2) | collective-permute-done | bytes 196640 | tf_op jit(solution)/shard_map/ppermute | solution.py:394
  22.9 2.9 %collective-permute-start.10 = (bf16[384,128]{1,0:T(8,128)(2,1)S(1)}, bf16[384,128]{1,0:T(8,128)(2,1)S(1)}, u32[]{:S(2)}, u32[]{:S(2)}) collective-permute-start(bf16[384,128]{1,0:T(8,128)(2,1)S(1)} %get-tuple-element.44), channel_id=1, source_target_pairs={{0,8},{8,0},{4,12},{12,4},{1,9},{9,1},{5,13},{13,5},{2,10},{10,2},... | collective-permute-start | bytes 294920 | tf_op jit(solution)/shard_map/ppermute | solution.py:402
  25.9 7.4 %collective-permute-done.10.refs_0_.query_ref = bf16[384,128]{1,0:T(8,128)(2,1)S(1)} collective-permute-done((bf16[384,128]{1,0:T(8,128)(2,1)S(1)}, bf16[384,128]{1,0:T(8,128)(2,1)S(1)}, u32[]{:S(2)}, u32[]{:S(2)}) %collective-permute-start.10) | collective-permute-done | bytes 98336 | tf_op jit(solution)/shard_map/ppermute | solution.py:402
  33.3 0.8 %shard_map.102 = (f32[8,384]{1,0:T(8,128)S(1)}, f32[128,384]{1,0:T(8,128)S(1)}) custom-call(bf16[384,128]{1,0:T(8,128)(2,1)S(1)} %collective-permute-done.10.refs_0_.query_ref, bf16[768,128]{1,0:T(8,128)(2,1)S(1)} %shard_map.96.refs_2_.refs_1_, bf16[128,768]{1,0:T(8,128)(2,1)S(1)} %shard_map.97.refs_3_.refs_2_), custom_call_target="tpu_custom_call" | custom-call | flops 150994944 | bytes 491520 | tf_op jit(solution)/shard_map/pallas_call | solution.py:26
  34.1 0.6 %shard_map.103 = (f32[8,384]{1,0:T(8,128)S(1)}, bf16[768,384]{1,0:T(8,128)(2,1)S(1)}) custom-call(bf16[384,128]{1,0:T(8,128)(2,1)S(1)} %collective-permute-done.10.refs_0_.query_ref, bf16[768,128]{1,0:T(8,128)(2,1)S(1)} %collective-permute-done.5.refs_4_.key_ref, f32[8,384]{1,0:T(8,128)S(1)} %get-tuple-element.45.given_ref), custom_call_target="tpu_custom_call" | custom-call | flops 75497472 | bytes 307200 | tf_op jit(solution)/shard_map/pallas_call | solution.py:26
  35.0 0.8 %shard_map.99 = (f32[8,384]{1,0:T(8,128)S(1)}, f32[128,384]{1,0:T(8,128)S(1)}) custom-call(bf16[384,128]{1,0:T(8,128)(2,1)S(1)} %collective-permute-done.7.refs_0_.query_ref, bf16[768,128]{1,0:T(8,128)(2,1)S(1)} %shard_map.96.refs_2_.refs_1_, bf16[128,768]{1,0:T(8,128)(2,1)S(1)} %shard_map.97.refs_3_.refs_2_), custom_call_target="tpu_custom_call" | custom-call | flops 150994944 | bytes 491520 | tf_op jit(solution)/shard_map/pallas_call | solution.py:26
  37.0 3.0 %collective-permute-start.9 = (bf16[128,384]{1,0:T(8,128)(2,1)S(1)}, bf16[128,384]{1,0:T(8,128)(2,1)S(1)}, u32[]{:S(2)}, u32[]{:S(2)}) collective-permute-start(bf16[128,384]{1,0:T(8,128)(2,1)S(1)} %shard_map.101), channel_id=1, source_target_pairs={{0,8},{8,0},{4,12},{12,4},{1,9},{9,1},{5,13},{13,5},{2,10},{10,2},... | collective-permute-start | bytes 294920 | tf_op jit(solution)/shard_map/ppermute | solution.py:413
  40.7 2.9 %collective-permute-start.8 = (f32[8,384]{1,0:T(8,128)S(1)}, f32[8,384]{1,0:T(8,128)S(1)}, u32[]{:S(2)}, u32[]{:S(2)}) collective-permute-start(f32[8,384]{1,0:T(8,128)S(1)} %get-tuple-element.41.stats_ref), channel_id=1, source_target_pairs={{0,8},{8,0},{4,12},{12,4},{1,9},{9,1},{5,13},{13,5},{2,10},{10,2},... | collective-permute-start | bytes 36872 | tf_op jit(solution)/shard_map/ppermute | solution.py:411
  43.6 0.7 %shard_map.98 = (f32[8,768]{1,0:T(8,128)S(1)}, f32[128,768]{1,0:T(8,128)S(1)}) custom-call(s32[6]{0:T(128)S(1)} %copy-done.7, bf16[768,128]{1,0:T(8,128)(2,1)S(1)} %get-tuple-element.32.refs_1_, bf16[768,128]{1,0:T(8,128)(2,1)S(1)} %shard_map.96.refs_2_.refs_1_, bf16[128,768]{1,0:T(8,128)(2,1)S(1)} %shard_map.97.refs_3_.refs_2_, ...), custom_call_target="tpu_custom_call" | custom-call | flops 603979776 | bytes 983064 | tf_op jit(solution)/shard_map/pallas_call | solution.py:26
  44.3 5.0 %collective-permute-done.11.refs_4_ = f32[8,384]{1,0:T(8,128)S(1)} collective-permute-done((f32[8,384]{1,0:T(8,128)S(1)}, f32[8,384]{1,0:T(8,128)S(1)}, u32[]{:S(2)}, u32[]{:S(2)}) %collective-permute-start.11) | collective-permute-done | bytes 12320 | tf_op jit(solution)/shard_map/ppermute | solution.py:411
  49.4 0.9 %shard_map.105 = bf16[768,128]{1,0:T(8,128)(2,1)} custom-call(bf16[768,128]{1,0:T(8,128)(2,1)S(1)} %get-tuple-element.27.stale_ref, f32[8,768]{1,0:T(8,128)S(1)} %get-tuple-element.28.fresh_ref, f32[8,768]{1,0:T(8,128)S(1)} %get-tuple-element.37.refs_0_, f32[128,768]{1,0:T(8,128)S(1)} %get-tuple-element.38.refs_1_, ...), custom_call_target="tpu_custom_call" | custom-call | flops 786432 | bytes 860160 | tf_op jit(solution)/shard_map/pallas_call | solution.py:26
  (37 shorter events, 4.2 us)
Async XLA Ops:
  0.0 4.3 %copy-start.1 = (bf16[768,1536]{1,0:T(8,128)(2,1)S(1)}, bf16[768,1536]{1,0:T(8,128)(2,1)}, u32[]{:S(2)}) copy-start(bf16[768,1536]{1,0:T(8,128)(2,1)} %own_ref.5) | copy-start | bytes 7077892
  0.0 7.8 %copy-start = (bf16[1536,768]{1,0:T(8,128)(2,1)S(1)}, bf16[1536,768]{1,0:T(8,128)(2,1)}, u32[]{:S(2)}) copy-start(bf16[1536,768]{1,0:T(8,128)(2,1)} %weight_ref.7) | copy-start | bytes 7077892
  0.0 7.8 %copy-start.3 = (f32[3072]{0:T(1024)S(1)}, f32[3072]{0:T(1024)}, u32[]{:S(2)}) copy-start(f32[3072]{0:T(1024)} %param.12) | copy-start | bytes 36868
  0.0 7.8 %copy-start.4 = (f32[3072]{0:T(1024)S(1)}, f32[3072]{0:T(1024)}, u32[]{:S(2)}) copy-start(f32[3072]{0:T(1024)} %param.11) | copy-start | bytes 36868
  0.0 7.8 %collective-permute-start = (bf16[768,1536]{1,0:T(8,128)(2,1)}, bf16[768,1536]{1,0:T(8,128)(2,1)S(1)}, u32[]{:S(2)}, u32[]{:S(2)}) collective-permute-start(bf16[768,1536]{1,0:T(8,128)(2,1)} %own_ref.5), channel_id=1, source_target_pairs={{0,1},{1,0},{2,3},{3,2},{4,5},{5,4},{6,7},{7,6},{8,9},{9,8},{10,11... | collective-permute-start | bytes 7077896 | tf_op jit(solution)/shard_map/ppermute | solution.py:385
  1.9 12.4 %collective-permute-start.3 = (bf16[1536,128]{1,0:T(8,128)(2,1)S(1)}, bf16[1536,128]{1,0:T(8,128)(2,1)S(1)}, u32[]{:S(2)}, u32[]{:S(2)}) collective-permute-start(bf16[1536,128]{1,0:T(8,128)(2,1)S(1)} %foreign_keys.1), channel_id=1, source_target_pairs={{0,2},{2,0},{1,3},{3,1},{4,6},{6,4},{5,7},{7,5},{8,10},{10,8},{9,1... | collective-permute-start | bytes 1179656 | tf_op jit(solution)/shard_map/ppermute | solution.py:386
  5.9 1.8 %collective-permute-start.1 = (f32[768,2]{1,0:T(8,128)S(1)}, f32[768,2]{1,0:T(8,128)S(1)}, u32[]{:S(2)}, u32[]{:S(2)}) collective-permute-start(f32[768,2]{1,0:T(8,128)S(1)} %moments.1.near_ref), channel_id=1, source_target_pairs={{0,1},{1,0},{2,3},{3,2},{4,5},{5,4},{6,7},{7,6},{8,9},{9,8},{10,11... | collective-permute-start | bytes 18440 | tf_op jit(solution)/shard_map/ppermute | solution.py:388
  9.2 9.3 %collective-permute-start.4 = (bf16[768,128]{1,0:T(8,128)(2,1)S(1)}, bf16[768,128]{1,0:T(8,128)(2,1)S(1)}, u32[]{:S(2)}, u32[]{:S(2)}) collective-permute-start(bf16[768,128]{1,0:T(8,128)(2,1)S(1)} %get-tuple-element.36), channel_id=1, source_target_pairs={{0,2},{2,0},{1,3},{3,1},{4,6},{6,4},{5,7},{7,5},{8,10},{10,8},{9,1... | collective-permute-start | bytes 589832 | tf_op jit(solution)/shard_map/ppermute | solution.py:395
  9.9 12.8 %collective-permute-start.2 = (bf16[768,128]{1,0:T(8,128)(2,1)S(1)}, bf16[768,128]{1,0:T(8,128)(2,1)S(1)}, u32[]{:S(2)}, u32[]{:S(2)}) collective-permute-start(bf16[768,128]{1,0:T(8,128)(2,1)S(1)} %get-tuple-element.31), channel_id=1, source_target_pairs={{0,2},{2,0},{1,3},{3,1},{4,6},{6,4},{5,7},{7,5},{8,10},{10,8},{9,1... | collective-permute-start | bytes 589832 | tf_op jit(solution)/shard_map/ppermute | solution.py:394
  11.3 3.0 %copy-start.5 = (f32[1,128]{1,0:T(1,128)S(1)}, f32[1,128]{1,0:T(1,128)}, u32[]{:S(2)}) copy-start(f32[1,128]{1,0:T(1,128)} %gain_ref.5) | copy-start | bytes 1540
  15.1 7.5 %copy-start.8 = (f32[1,128]{1,0:T(1,128)S(1)}, f32[1,128]{1,0:T(1,128)}, u32[]{:S(2)}) copy-start(f32[1,128]{1,0:T(1,128)} %gain_ref.3) | copy-start | bytes 1540
  15.2 18.9 %collective-permute-start.5 = (bf16[768,128]{1,0:T(8,128)(2,1)S(1)}, bf16[768,128]{1,0:T(8,128)(2,1)S(1)}, u32[]{:S(2)}, u32[]{:S(2)}) collective-permute-start(bf16[768,128]{1,0:T(8,128)(2,1)S(1)} %shard_map.96.refs_2_.refs_1_), channel_id=1, source_target_pairs={{0,4},{4,0},{8,12},{12,8},{1,5},{5,1},{9,13},{13,9},{2,6},{6,2},{1... | collective-permute-start | bytes 589832 | tf_op jit(solution)/shard_map/ppermute | solution.py:399
  18.6 21.4 %copy-start.2 = (bf16[768,128]{1,0:T(8,128)(2,1)S(1)}, bf16[768,128]{1,0:T(8,128)(2,1)}, u32[]{:S(2)}) copy-start(bf16[768,128]{1,0:T(8,128)(2,1)} %cached_ref.1) | copy-start | bytes 589828
  18.6 21.4 %copy-start.6 = (s32[6]{0:T(128)S(1)}, s32[6]{0:T(128)}, u32[]{:S(2)}) copy-start(s32[6]{0:T(128)} %slot_ref.1) | copy-start | bytes 76
  18.6 21.3 %copy-start.7 = (s32[6]{0:T(128)S(1)}, s32[6]{0:T(128)}, u32[]{:S(2)}) copy-start(s32[6]{0:T(128)} %refs_0_.1) | copy-start | bytes 76
  18.7 17.7 %collective-permute-start.6 = (bf16[128,768]{1,0:T(8,128)(2,1)S(1)}, bf16[128,768]{1,0:T(8,128)(2,1)S(1)}, u32[]{:S(2)}, u32[]{:S(2)}) collective-permute-start(bf16[128,768]{1,0:T(8,128)(2,1)S(1)} %shard_map.97.refs_3_.refs_2_), channel_id=1, source_target_pairs={{0,4},{4,0},{8,12},{12,8},{1,5},{5,1},{9,13},{13,9},{2,6},{6,2},{1... | collective-permute-start | bytes 589832 | tf_op jit(solution)/shard_map/ppermute | solution.py:404
  22.9 10.4 %collective-permute-start.10 = (bf16[384,128]{1,0:T(8,128)(2,1)S(1)}, bf16[384,128]{1,0:T(8,128)(2,1)S(1)}, u32[]{:S(2)}, u32[]{:S(2)}) collective-permute-start(bf16[384,128]{1,0:T(8,128)(2,1)S(1)} %get-tuple-element.44), channel_id=1, source_target_pairs={{0,8},{8,0},{4,12},{12,4},{1,9},{9,1},{5,13},{13,5},{2,10},{10,2},... | collective-permute-start | bytes 294920 | tf_op jit(solution)/shard_map/ppermute | solution.py:402
  25.8 9.2 %collective-permute-start.7 = (bf16[384,128]{1,0:T(8,128)(2,1)S(1)}, bf16[384,128]{1,0:T(8,128)(2,1)S(1)}, u32[]{:S(2)}, u32[]{:S(2)}) collective-permute-start(bf16[384,128]{1,0:T(8,128)(2,1)S(1)} %get-tuple-element.39), channel_id=1, source_target_pairs={{0,8},{8,0},{4,12},{12,4},{1,9},{9,1},{5,13},{13,5},{2,10},{10,2},... | collective-permute-start | bytes 294920 | tf_op jit(solution)/shard_map/ppermute | solution.py:402
  36.7 12.7 %collective-permute-start.12 = (bf16[128,384]{1,0:T(8,128)(2,1)S(1)}, bf16[128,384]{1,0:T(8,128)(2,1)S(1)}, u32[]{:S(2)}, u32[]{:S(2)}) collective-permute-start(bf16[128,384]{1,0:T(8,128)(2,1)S(1)} %shard_map.104), channel_id=1, source_target_pairs={{0,8},{8,0},{4,12},{12,4},{1,9},{9,1},{5,13},{13,5},{2,10},{10,2},... | collective-permute-start | bytes 294920 | tf_op jit(solution)/shard_map/ppermute | solution.py:413
  37.0 12.4 %collective-permute-start.9 = (bf16[128,384]{1,0:T(8,128)(2,1)S(1)}, bf16[128,384]{1,0:T(8,128)(2,1)S(1)}, u32[]{:S(2)}, u32[]{:S(2)}) collective-permute-start(bf16[128,384]{1,0:T(8,128)(2,1)S(1)} %shard_map.101), channel_id=1, source_target_pairs={{0,8},{8,0},{4,12},{12,4},{1,9},{9,1},{5,13},{13,5},{2,10},{10,2},... | collective-permute-start | bytes 294920 | tf_op jit(solution)/shard_map/ppermute | solution.py:413
  40.6 8.7 %collective-permute-start.11 = (f32[8,384]{1,0:T(8,128)S(1)}, f32[8,384]{1,0:T(8,128)S(1)}, u32[]{:S(2)}, u32[]{:S(2)}) collective-permute-start(f32[8,384]{1,0:T(8,128)S(1)} %get-tuple-element.46.stats_ref), channel_id=1, source_target_pairs={{0,8},{8,0},{4,12},{12,4},{1,9},{9,1},{5,13},{13,5},{2,10},{10,2},... | collective-permute-start | bytes 36872 | tf_op jit(solution)/shard_map/ppermute | solution.py:411
  40.7 8.7 %collective-permute-start.8 = (f32[8,384]{1,0:T(8,128)S(1)}, f32[8,384]{1,0:T(8,128)S(1)}, u32[]{:S(2)}, u32[]{:S(2)}) collective-permute-start(f32[8,384]{1,0:T(8,128)S(1)} %get-tuple-element.41.stats_ref), channel_id=1, source_target_pairs={{0,8},{8,0},{4,12},{12,4},{1,9},{9,1},{5,13},{13,5},{2,10},{10,2},... | collective-permute-start | bytes 36872 | tf_op jit(solution)/shard_map/ppermute | solution.py:411

commit v2 on v1

--- a/solution.py
+++ b/solution.py
@@ -223,9 +223,21 @@
     )
 
 
+def for_groups(groups, active_ref, body):
+    for index in range(groups):
+        if active_ref is None:
+            body(index)
+        else:
+            blocks = active_ref.shape[0]
+            here = [
+                (active_ref[at] >= 0) & (active_ref[at] * groups // blocks == index)
+                for at in range(blocks)
+            ]
+            pl.when(functools.reduce(jnp.logical_or, here))(functools.partial(body, index))
+
+
 def attend_kernel(groups, spans, divide, listed, *refs):
-    if listed:
-        active_ref, refs = refs[0], refs[1:]
+    active_ref, refs = (refs[0], refs[1:]) if listed else (None, refs)
     query_ref, refs = refs[0], refs[1:]
     span_refs, refs = refs[: 2 * spans], refs[2 * spans :]
     stats_ref, mixed_ref = refs
@@ -259,14 +271,7 @@
         stats_ref[1:2, cols] = total
         mixed_ref[:, cols] = mixed / total if divide else mixed
 
-    for index in range(groups):
-        if listed:
-            blocks = active_ref.shape[0]
-            here = [active_ref[at] * groups // blocks == index for at in range(blocks)]
-            here = [hit & (active_ref[at] >= 0) for at, hit in enumerate(here)]
-            pl.when(functools.reduce(jnp.logical_or, here))(functools.partial(pair, index))
-        else:
-            pair(index)
+    for_groups(groups, active_ref, pair)
 
 
 def attend(groups, queries, spans, divide, active=None):
@@ -282,11 +287,14 @@
     )
 
 
-def peek_kernel(groups, query_ref, key_ref, given_ref, stats_ref, weights_ref):
+def peek_kernel(groups, listed, *refs):
+    active_ref, refs = (refs[0], refs[1:]) if listed else (None, refs)
+    query_ref, key_ref, given_ref, stats_ref, weights_ref = refs
     head_dim = query_ref.shape[1]
     width = query_ref.shape[0] // groups
     factor = head_dim ** (-0.5) * 1.4426950408889634
-    for index in range(groups):
+
+    def group(index):
         cols = slice(index * width, (index + 1) * width)
         scores = lax.dot_general(
             key_ref[...], query_ref[cols, :], (((1,), (1,)), ((), ())),
@@ -303,12 +311,16 @@
         stats_ref[2:3, cols] = shrink
         weights_ref[:, cols] = weights.astype(jnp.bfloat16)
 
-
-def peek(groups, queries, keys, given):
-    return call(
-        functools.partial(peek_kernel, groups),
+    for_groups(groups, active_ref, group)
+
+
+def peek(groups, queries, keys, given, active=None):
+    listed = () if active is None else (active,)
+    return call(
+        functools.partial(peek_kernel, groups, bool(listed)),
         (shape(given.shape, jnp.float32), shape((keys.shape[0], queries.shape[0]), jnp.bfloat16)),
-        (queries, keys, given), 2 * queries.size * keys.shape[0],
+        (*listed, queries, keys, given), 2 * queries.size * keys.shape[0],
+        scalars=len(listed),
     )
 
 
@@ -319,9 +331,9 @@
     ).astype(out_ref.dtype)
 
 
-def close(stats, weights, values, mixed):
-    return call(
-        close_kernel, shape(mixed.shape, jnp.bfloat16), (stats, weights, values, mixed),
+def close(stats, weights, values, mixed, dtype):
+    return call(
+        close_kernel, shape(mixed.shape, dtype), (stats, weights, values, mixed),
         2 * values.size * weights.shape[1],
     )
 
@@ -404,15 +416,18 @@
     beside_values = lax.ppermute(values, "seq", beside)
 
     stale, fresh = stale_rows(active, cache_slot, cached)
+    own_stats, own_mixed = attend(
+        blocks // 2, queries, [(keys, values)], False, active=active
+    )
     returned = []
     for visiting in visitors:
         stats, mixed = attend(1, visiting, [(keys, values)], False)
         stats, weights = peek(1, visiting, beside_keys, stats)
         got_stats = lax.ppermute(stats, "seq", across)
-        lent = close(stats, weights, beside_values, mixed)
+        lent = close(stats, weights, beside_values, mixed, jnp.bfloat16)
         returned.append((got_stats, lax.ppermute(lent, "seq", across)))
-    spans = [(keys, values), (beside_keys, beside_values)]
-    own = attend(blocks // 2, queries, spans, True, active=active)
+    stats, weights = peek(blocks // 2, queries, beside_keys, own_stats, active=active)
+    own = (stats, close(stats, weights, beside_values, own_mixed, jnp.float32))
     return blend(stale, fresh, [[own], returned])
 
 

time: 50.4 us -> 50.9 us (level)
  the two profiles are of different devices: /device:TPU:0 before, /device:TPU:8 now
where the time goes in v2:
time: 50.9 us; the launch traced here: 50.7 us
  waiting for transfers between devices  19.1 us (38%)
  Pallas kernels  17.4 us (34%)
  starting transfers between devices  13.9 us (27%)
    pallas_call x17, Pallas kernels, call(): pl.pallas_call(body, out_shape=out, in_specs=[SMEM] * scalars + [VMEM] *...  14.6 us
    ppermute x2, waiting for transfers between devices, swapped_plan(): visitors = [lax.ppermute(half, 'seq', across) for half in halves]  6.55 us
    ppermute x1, waiting for transfers between devices, swapped_plan(): got_query = lax.ppermute(part_query, 'fsdp', swap)  3.68 us
    ppermute x2, starting transfers between devices, swapped_plan(): returned.append((got_stats, lax.ppermute(lent, 'seq', across)))  3.53 us
    ppermute x2, waiting for transfers between devices, swapped_plan(): got_stats = lax.ppermute(stats, 'seq', across)  3.15 us
    ppermute x2, starting transfers between devices, swapped_plan(): got_stats = lax.ppermute(stats, 'seq', across)  2.99 us
    ppermute x2, starting transfers between devices, swapped_plan(): visitors = [lax.ppermute(half, 'seq', across) for half in halves]  2.99 us
    ppermute x1, waiting for transfers between devices, swapped_plan(): got_value = lax.ppermute(part_value, 'fsdp', swap)  2.44 us
  transfers between devices with their start and end apart: 13, of which 8 were waited for; matrix products, arithmetic and copies ran while one was open for 0% of the time, Pallas kernels for 32%

profile of v2, /device:TPU:8, one launch (start us, length us, event | category | flops | bytes accessed | tf_op | source)
XLA Modules:
  0.0 50.7 jit_solution(8678213963922850906)
XLA Ops:
  0.1 1.2 %foreign_keys.1 = bf16[1536,128]{1,0:T(8,128)(2,1)S(1)} custom-call(bf16[1536,768]{1,0:T(8,128)(2,1)} %weight_ref.7), custom_call_target="tpu_custom_call" | custom-call | bytes 786432 | tf_op jit(solution)/shard_map/foreign_keys/pallas_call | solution.py:168
  1.3 1.6 %collective-permute-start.3 = (bf16[1536,128]{1,0:T(8,128)(2,1)S(1)}, bf16[1536,128]{1,0:T(8,128)(2,1)S(1)}, u32[]{:S(2)}, u32[]{:S(2)}) collective-permute-start(bf16[1536,128]{1,0:T(8,128)(2,1)S(1)} %foreign_keys.1), channel_id=1, source_target_pairs={{0,2},{2,0},{1,3},{3,1},{4,6},{6,4},{5,7},{7,5},{8,10},{10,8},{9,1... | collective-permute-start | bytes 1179656 | tf_op jit(solution)/shard_map/ppermute | solution.py:398
  2.8 1.6 %moments.1.near_ref = f32[768,2]{1,0:T(8,128)S(1)} custom-call(bf16[768,1536]{1,0:T(8,128)(2,1)S(1)} %copy-done.1), custom_call_target="tpu_custom_call" | custom-call | flops 5898240 | bytes 2359296 | tf_op jit(solution)/shard_map/moments/pallas_call | solution.py:59
  5.0 1.3 %collective-permute-done.1.far_ref = f32[768,2]{1,0:T(8,128)S(1)} collective-permute-done((f32[768,2]{1,0:T(8,128)S(1)}, f32[768,2]{1,0:T(8,128)S(1)}, u32[]{:S(2)}, u32[]{:S(2)}) %collective-permute-start.1) | collective-permute-done | bytes 6176 | tf_op jit(solution)/shard_map/ppermute | solution.py:400
  6.3 1.4 %shard_map.92 = (bf16[768,1536]{1,0:T(8,128)(2,1)S(1)}, bf16[768,128]{1,0:T(8,128)(2,1)S(1)}, bf16[768,128]{1,0:T(8,128)(2,1)S(1)}) custom-call(bf16[768,1536]{1,0:T(8,128)(2,1)S(1)} %copy-done.1, bf16[768,1536]{1,0:T(8,128)(2,1)S(1)} %collective-permute-done.other_ref, f32[768,2]{1,0:T(8,128)S(1)} %moments.1.near_ref, ...), custom_call_target="tpu_custom_call" | custom-call | flops 603979776 | bytes 7114752 | tf_op jit(solution)/shard_map/pallas_call | solution.py:26
  8.4 1.4 %collective-permute-start.2 = (bf16[768,128]{1,0:T(8,128)(2,1)S(1)}, bf16[768,128]{1,0:T(8,128)(2,1)S(1)}, u32[]{:S(2)}, u32[]{:S(2)}) collective-permute-start(bf16[768,128]{1,0:T(8,128)(2,1)S(1)} %get-tuple-element.33), channel_id=1, source_target_pairs={{0,2},{2,0},{1,3},{3,1},{4,6},{6,4},{5,7},{7,5},{8,10},{10,8},{9,1... | collective-permute-start | bytes 589832 | tf_op jit(solution)/shard_map/ppermute | solution.py:406
  9.8 1.6 %shard_map.95 = (bf16[768,1536]{1,0:T(8,128)(2,1)S(1)}, f32[768,128]{1,0:T(8,128)S(1)}) custom-call(bf16[768,1536]{1,0:T(8,128)(2,1)S(1)} %copy-done.1, bf16[768,1536]{1,0:T(8,128)(2,1)S(1)} %collective-permute-done.other_ref, f32[768,2]{1,0:T(8,128)S(1)} %moments.1.near_ref, f32[768,2]{1,0:T(8,128)S(1)} %collective-permute-done.1.far_ref, ...), custom_call_target="tpu_custom_call" | custom-call | flops 301989888 | bytes 9474048 | tf_op jit(solution)/shard_map/pallas_call | solution.py:26
  11.4 1.9 %collective-permute-done.3.weight_ref = bf16[1536,128]{1,0:T(8,128)(2,1)S(1)} collective-permute-done((bf16[1536,128]{1,0:T(8,128)(2,1)S(1)}, bf16[1536,128]{1,0:T(8,128)(2,1)S(1)}, u32[]{:S(2)}, u32[]{:S(2)}) %collective-permute-start.3) | collective-permute-done | bytes 393248 | tf_op jit(solution)/shard_map/ppermute | solution.py:398
  13.3 0.9 %shard_map.96.refs_2_.refs_1_ = bf16[768,128]{1,0:T(8,128)(2,1)S(1)} custom-call(f32[768,128]{1,0:T(8,128)S(1)} %get-tuple-element.35.kept_ref, bf16[768,1536]{1,0:T(8,128)(2,1)S(1)} %get-tuple-element.36.normed_ref, bf16[1536,128]{1,0:T(8,128)(2,1)S(1)} %collective-permute-done.3.weight_ref, f32[1,128]{1,0:T(1,128)S(1)} %copy-done.5), custom_call_target="tpu_custom_call" | custom-call | flops 301989888 | bytes 3146240 | tf_op jit(solution)/shard_map/pallas_call | solution.py:26
  14.3 0.8 %shard_map.93 = (f32[768,128]{1,0:T(8,128)S(1)}, f32[768,128]{1,0:T(8,128)S(1)}) custom-call(bf16[768,1536]{1,0:T(8,128)(2,1)S(1)} %get-tuple-element.31.normed_ref.refs_0_, bf16[1536,768]{1,0:T(8,128)(2,1)S(1)} %copy-done), custom_call_target="tpu_custom_call" | custom-call | flops 603979776 | bytes 4718592 | tf_op jit(solution)/shard_map/pallas_call | solution.py:26
  15.1 2.4 %collective-permute-done.5.got_ref = bf16[768,128]{1,0:T(8,128)(2,1)S(1)} collective-permute-done((bf16[768,128]{1,0:T(8,128)(2,1)S(1)}, bf16[768,128]{1,0:T(8,128)(2,1)S(1)}, u32[]{:S(2)}, u32[]{:S(2)}) %collective-permute-start.5) | collective-permute-done | bytes 196640 | tf_op jit(solution)/shard_map/ppermute | solution.py:407
  17.8 3.7 %collective-permute-done.2.got_ref = bf16[768,128]{1,0:T(8,128)(2,1)S(1)} collective-permute-done((bf16[768,128]{1,0:T(8,128)(2,1)S(1)}, bf16[768,128]{1,0:T(8,128)(2,1)S(1)}, u32[]{:S(2)}, u32[]{:S(2)}) %collective-permute-start.2) | collective-permute-done | bytes 196640 | tf_op jit(solution)/shard_map/ppermute | solution.py:406
  21.7 2.7 %collective-permute-start.10 = (bf16[384,128]{1,0:T(8,128)(2,1)S(1)}, bf16[384,128]{1,0:T(8,128)(2,1)S(1)}, u32[]{:S(2)}, u32[]{:S(2)}) collective-permute-start(bf16[384,128]{1,0:T(8,128)(2,1)S(1)} %get-tuple-element.48), channel_id=1, source_target_pairs={{0,8},{8,0},{4,12},{12,4},{1,9},{9,1},{5,13},{13,5},{2,10},{10,2},... | collective-permute-start | bytes 294920 | tf_op jit(solution)/shard_map/ppermute | solution.py:414
  24.7 5.9 %collective-permute-done.10.refs_0_ = bf16[384,128]{1,0:T(8,128)(2,1)S(1)} collective-permute-done((bf16[384,128]{1,0:T(8,128)(2,1)S(1)}, bf16[384,128]{1,0:T(8,128)(2,1)S(1)}, u32[]{:S(2)}, u32[]{:S(2)}) %collective-permute-start.10) | collective-permute-done | bytes 98336 | tf_op jit(solution)/shard_map/ppermute | solution.py:414
  30.6 0.8 %shard_map.104 = (f32[8,384]{1,0:T(8,128)S(1)}, f32[128,384]{1,0:T(8,128)S(1)}) custom-call(bf16[384,128]{1,0:T(8,128)(2,1)S(1)} %collective-permute-done.10.refs_0_, bf16[768,128]{1,0:T(8,128)(2,1)S(1)} %shard_map.96.refs_2_.refs_1_, bf16[128,768]{1,0:T(8,128)(2,1)S(1)} %shard_map.97.refs_3_.refs_2_), custom_call_target="tpu_custom_call" | custom-call | flops 150994944 | bytes 491520 | tf_op jit(solution)/shard_map/pallas_call | solution.py:26
  32.6 0.8 %shard_map.101 = (f32[8,384]{1,0:T(8,128)S(1)}, f32[128,384]{1,0:T(8,128)S(1)}) custom-call(bf16[384,128]{1,0:T(8,128)(2,1)S(1)} %collective-permute-done.7.refs_0_, bf16[768,128]{1,0:T(8,128)(2,1)S(1)} %shard_map.96.refs_2_.refs_1_, bf16[128,768]{1,0:T(8,128)(2,1)S(1)} %shard_map.97.refs_3_.refs_2_), custom_call_target="tpu_custom_call" | custom-call | flops 150994944 | bytes 491520 | tf_op jit(solution)/shard_map/pallas_call | solution.py:26
  34.3 3.4 %collective-permute-start.12 = (bf16[128,384]{1,0:T(8,128)(2,1)S(1)}, bf16[128,384]{1,0:T(8,128)(2,1)S(1)}, u32[]{:S(2)}, u32[]{:S(2)}) collective-permute-start(bf16[128,384]{1,0:T(8,128)(2,1)S(1)} %shard_map.106), channel_id=1, source_target_pairs={{0,8},{8,0},{4,12},{12,4},{1,9},{9,1},{5,13},{13,5},{2,10},{10,2},... | collective-permute-start | bytes 294920 | tf_op jit(solution)/shard_map/ppermute | solution.py:428
  38.7 2.6 %shard_map.98 = (f32[8,768]{1,0:T(8,128)S(1)}, f32[128,768]{1,0:T(8,128)S(1)}) custom-call(s32[6]{0:T(128)S(1)} %copy-done.7, bf16[768,128]{1,0:T(8,128)(2,1)S(1)} %get-tuple-element.34.refs_1_, bf16[768,128]{1,0:T(8,128)(2,1)S(1)} %shard_map.96.refs_2_.refs_1_, bf16[128,768]{1,0:T(8,128)(2,1)S(1)} %shard_map.97.refs_3_.refs_2_), custom_call_target="tpu_custom_call" | custom-call | flops 301989888 | bytes 589848 | tf_op jit(solution)/shard_map/pallas_call | solution.py:26
  41.3 2.0 %shard_map.99 = (f32[8,768]{1,0:T(8,128)S(1)}, bf16[768,768]{1,0:T(8,128)(2,1)S(1)}) custom-call(s32[6]{0:T(128)S(1)} %copy-done.7, bf16[768,128]{1,0:T(8,128)(2,1)S(1)} %get-tuple-element.34.refs_1_, bf16[768,128]{1,0:T(8,128)(2,1)S(1)} %collective-permute-done.4.refs_2_.refs_1_, f32[8,768]{1,0:T(8,128)S(1)} %get-tuple-element.39.refs_3_), custom_call_target="tpu_custom_call" | custom-call | flops 150994944 | bytes 417816 | tf_op jit(solution)/shard_map/pallas_call | solution.py:26
  43.4 1.9 %collective-permute-start.11 = (f32[8,384]{1,0:T(8,128)S(1)}, f32[8,384]{1,0:T(8,128)S(1)}, u32[]{:S(2)}, u32[]{:S(2)}) collective-permute-start(f32[8,384]{1,0:T(8,128)S(1)} %get-tuple-element.50.stats_ref), channel_id=1, source_target_pairs={{0,8},{8,0},{4,12},{12,4},{1,9},{9,1},{5,13},{13,5},{2,10},{10,2},... | collective-permute-start | bytes 36872 | tf_op jit(solution)/shard_map/ppermute | solution.py:426
  45.2 1.1 %collective-permute-start.8 = (f32[8,384]{1,0:T(8,128)S(1)}, f32[8,384]{1,0:T(8,128)S(1)}, u32[]{:S(2)}, u32[]{:S(2)}) collective-permute-start(f32[8,384]{1,0:T(8,128)S(1)} %get-tuple-element.45.stats_ref), channel_id=1, source_target_pairs={{0,8},{8,0},{4,12},{12,4},{1,9},{9,1},{5,13},{13,5},{2,10},{10,2},... | collective-permute-start | bytes 36872 | tf_op jit(solution)/shard_map/ppermute | solution.py:426
  46.7 1.4 %collective-permute-done.11.refs_4_ = f32[8,384]{1,0:T(8,128)S(1)} collective-permute-done((f32[8,384]{1,0:T(8,128)S(1)}, f32[8,384]{1,0:T(8,128)S(1)}, u32[]{:S(2)}, u32[]{:S(2)}) %collective-permute-start.11) | collective-permute-done | bytes 12320 | tf_op jit(solution)/shard_map/ppermute | solution.py:426
  48.1 1.7 %collective-permute-done.8.refs_2_ = f32[8,384]{1,0:T(8,128)S(1)} collective-permute-done((f32[8,384]{1,0:T(8,128)S(1)}, f32[8,384]{1,0:T(8,128)S(1)}, u32[]{:S(2)}, u32[]{:S(2)}) %collective-permute-start.8) | collective-permute-done | bytes 12320 | tf_op jit(solution)/shard_map/ppermute | solution.py:426
  49.9 0.9 %shard_map.107 = bf16[768,128]{1,0:T(8,128)(2,1)} custom-call(bf16[768,128]{1,0:T(8,128)(2,1)S(1)} %get-tuple-element.29.stale_ref, f32[8,768]{1,0:T(8,128)S(1)} %get-tuple-element.30.fresh_ref, f32[8,768]{1,0:T(8,128)S(1)} %get-tuple-element.40.stats_ref.refs_0_, f32[128,768]{1,0:T(8,128)S(1)} %shard_map.100.refs_1_, ...), custom_call_target="tpu_custom_call" | custom-call | flops 786432 | bytes 860160 | tf_op jit(solution)/shard_map/pallas_call | solution.py:26
  (39 shorter events, 5.5 us)
Async XLA Ops:
  0.0 2.8 %copy-start.1 = (bf16[768,1536]{1,0:T(8,128)(2,1)S(1)}, bf16[768,1536]{1,0:T(8,128)(2,1)}, u32[]{:S(2)}) copy-start(bf16[768,1536]{1,0:T(8,128)(2,1)} %own_ref.5) | copy-start | bytes 7077892
  0.0 6.3 %copy-start = (bf16[1536,768]{1,0:T(8,128)(2,1)S(1)}, bf16[1536,768]{1,0:T(8,128)(2,1)}, u32[]{:S(2)}) copy-start(bf16[1536,768]{1,0:T(8,128)(2,1)} %weight_ref.7) | copy-start | bytes 7077892
  0.0 6.3 %copy-start.3 = (f32[3072]{0:T(1024)S(1)}, f32[3072]{0:T(1024)}, u32[]{:S(2)}) copy-start(f32[3072]{0:T(1024)} %param.12) | copy-start | bytes 36868
  0.0 6.3 %copy-start.4 = (f32[3072]{0:T(1024)S(1)}, f32[3072]{0:T(1024)}, u32[]{:S(2)}) copy-start(f32[3072]{0:T(1024)} %param.11) | copy-start | bytes 36868
  0.0 6.3 %collective-permute-start = (bf16[768,1536]{1,0:T(8,128)(2,1)}, bf16[768,1536]{1,0:T(8,128)(2,1)S(1)}, u32[]{:S(2)}, u32[]{:S(2)}) collective-permute-start(bf16[768,1536]{1,0:T(8,128)(2,1)} %own_ref.5), channel_id=1, source_target_pairs={{0,1},{1,0},{2,3},{3,2},{4,5},{5,4},{6,7},{7,6},{8,9},{9,8},{10,11... | collective-permute-start | bytes 7077896 | tf_op jit(solution)/shard_map/ppermute | solution.py:397
  1.3 12.1 %collective-permute-start.3 = (bf16[1536,128]{1,0:T(8,128)(2,1)S(1)}, bf16[1536,128]{1,0:T(8,128)(2,1)S(1)}, u32[]{:S(2)}, u32[]{:S(2)}) collective-permute-start(bf16[1536,128]{1,0:T(8,128)(2,1)S(1)} %foreign_keys.1), channel_id=1, source_target_pairs={{0,2},{2,0},{1,3},{3,1},{4,6},{6,4},{5,7},{7,5},{8,10},{10,8},{9,1... | collective-permute-start | bytes 1179656 | tf_op jit(solution)/shard_map/ppermute | solution.py:398
  4.5 1.8 %collective-permute-start.1 = (f32[768,2]{1,0:T(8,128)S(1)}, f32[768,2]{1,0:T(8,128)S(1)}, u32[]{:S(2)}, u32[]{:S(2)}) collective-permute-start(f32[768,2]{1,0:T(8,128)S(1)} %moments.1.near_ref), channel_id=1, source_target_pairs={{0,1},{1,0},{2,3},{3,2},{4,5},{5,4},{6,7},{7,6},{8,9},{9,8},{10,11... | collective-permute-start | bytes 18440 | tf_op jit(solution)/shard_map/ppermute | solution.py:400
  7.7 9.8 %collective-permute-start.5 = (bf16[768,128]{1,0:T(8,128)(2,1)S(1)}, bf16[768,128]{1,0:T(8,128)(2,1)S(1)}, u32[]{:S(2)}, u32[]{:S(2)}) collective-permute-start(bf16[768,128]{1,0:T(8,128)(2,1)S(1)} %get-tuple-element.38), channel_id=1, source_target_pairs={{0,2},{2,0},{1,3},{3,1},{4,6},{6,4},{5,7},{7,5},{8,10},{10,8},{9,1... | collective-permute-start | bytes 589832 | tf_op jit(solution)/shard_map/ppermute | solution.py:407
  8.4 13.1 %collective-permute-start.2 = (bf16[768,128]{1,0:T(8,128)(2,1)S(1)}, bf16[768,128]{1,0:T(8,128)(2,1)S(1)}, u32[]{:S(2)}, u32[]{:S(2)}) collective-permute-start(bf16[768,128]{1,0:T(8,128)(2,1)S(1)} %get-tuple-element.33), channel_id=1, source_target_pairs={{0,2},{2,0},{1,3},{3,1},{4,6},{6,4},{5,7},{7,5},{8,10},{10,8},{9,1... | collective-permute-start | bytes 589832 | tf_op jit(solution)/shard_map/ppermute | solution.py:406
  9.8 3.5 %copy-start.5 = (f32[1,128]{1,0:T(1,128)S(1)}, f32[1,128]{1,0:T(1,128)}, u32[]{:S(2)}) copy-start(f32[1,128]{1,0:T(1,128)} %gain_ref.5) | copy-start | bytes 1540
  14.2 7.3 %copy-start.8 = (f32[1,128]{1,0:T(1,128)S(1)}, f32[1,128]{1,0:T(1,128)}, u32[]{:S(2)}) copy-start(f32[1,128]{1,0:T(1,128)} %gain_ref.3) | copy-start | bytes 1540
  14.2 17.2 %collective-permute-start.4 = (bf16[768,128]{1,0:T(8,128)(2,1)S(1)}, bf16[768,128]{1,0:T(8,128)(2,1)S(1)}, u32[]{:S(2)}, u32[]{:S(2)}) collective-permute-start(bf16[768,128]{1,0:T(8,128)(2,1)S(1)} %shard_map.96.refs_2_.refs_1_), channel_id=1, source_target_pairs={{0,4},{4,0},{8,12},{12,8},{1,5},{5,1},{9,13},{13,9},{2,6},{6,2},{1... | collective-permute-start | bytes 589832 | tf_op jit(solution)/shard_map/ppermute | solution.py:411
  17.7 20.4 %copy-start.2 = (bf16[768,128]{1,0:T(8,128)(2,1)S(1)}, bf16[768,128]{1,0:T(8,128)(2,1)}, u32[]{:S(2)}) copy-start(bf16[768,128]{1,0:T(8,128)(2,1)} %cached_ref.1) | copy-start | bytes 589828
  17.7 20.4 %copy-start.6 = (s32[6]{0:T(128)S(1)}, s32[6]{0:T(128)}, u32[]{:S(2)}) copy-start(s32[6]{0:T(128)} %slot_ref.1) | copy-start | bytes 76
  17.7 20.4 %copy-start.7 = (s32[6]{0:T(128)S(1)}, s32[6]{0:T(128)}, u32[]{:S(2)}) copy-start(s32[6]{0:T(128)} %refs_0_.3) | copy-start | bytes 76
  17.7 16.3 %collective-permute-start.6 = (bf16[128,768]{1,0:T(8,128)(2,1)S(1)}, bf16[128,768]{1,0:T(8,128)(2,1)S(1)}, u32[]{:S(2)}, u32[]{:S(2)}) collective-permute-start(bf16[128,768]{1,0:T(8,128)(2,1)S(1)} %shard_map.97.refs_3_.refs_2_), channel_id=1, source_target_pairs={{0,4},{4,0},{8,12},{12,8},{1,5},{5,1},{9,13},{13,9},{2,6},{6,2},{1... | collective-permute-start | bytes 589832 | tf_op jit(solution)/shard_map/ppermute | solution.py:416
  21.7 8.9 %collective-permute-start.10 = (bf16[384,128]{1,0:T(8,128)(2,1)S(1)}, bf16[384,128]{1,0:T(8,128)(2,1)S(1)}, u32[]{:S(2)}, u32[]{:S(2)}) collective-permute-start(bf16[384,128]{1,0:T(8,128)(2,1)S(1)} %get-tuple-element.48), channel_id=1, source_target_pairs={{0,8},{8,0},{4,12},{12,4},{1,9},{9,1},{5,13},{13,5},{2,10},{10,2},... | collective-permute-start | bytes 294920 | tf_op jit(solution)/shard_map/ppermute | solution.py:414
  24.3 8.3 %collective-permute-start.7 = (bf16[384,128]{1,0:T(8,128)(2,1)S(1)}, bf16[384,128]{1,0:T(8,128)(2,1)S(1)}, u32[]{:S(2)}, u32[]{:S(2)}) collective-permute-start(bf16[384,128]{1,0:T(8,128)(2,1)S(1)} %get-tuple-element.43), channel_id=1, source_target_pairs={{0,8},{8,0},{4,12},{12,4},{1,9},{9,1},{5,13},{13,5},{2,10},{10,2},... | collective-permute-start | bytes 294920 | tf_op jit(solution)/shard_map/ppermute | solution.py:414
  34.3 15.6 %collective-permute-start.12 = (bf16[128,384]{1,0:T(8,128)(2,1)S(1)}, bf16[128,384]{1,0:T(8,128)(2,1)S(1)}, u32[]{:S(2)}, u32[]{:S(2)}) collective-permute-start(bf16[128,384]{1,0:T(8,128)(2,1)S(1)} %shard_map.106), channel_id=1, source_target_pairs={{0,8},{8,0},{4,12},{12,4},{1,9},{9,1},{5,13},{13,5},{2,10},{10,2},... | collective-permute-start | bytes 294920 | tf_op jit(solution)/shard_map/ppermute | solution.py:428
  38.0 11.8 %collective-permute-start.9 = (bf16[128,384]{1,0:T(8,128)(2,1)S(1)}, bf16[128,384]{1,0:T(8,128)(2,1)S(1)}, u32[]{:S(2)}, u32[]{:S(2)}) collective-permute-start(bf16[128,384]{1,0:T(8,128)(2,1)S(1)} %shard_map.103), channel_id=1, source_target_pairs={{0,8},{8,0},{4,12},{12,4},{1,9},{9,1},{5,13},{13,5},{2,10},{10,2},... | collective-permute-start | bytes 294920 | tf_op jit(solution)/shard_map/ppermute | solution.py:428
  43.4 4.8 %collective-permute-start.11 = (f32[8,384]{1,0:T(8,128)S(1)}, f32[8,384]{1,0:T(8,128)S(1)}, u32[]{:S(2)}, u32[]{:S(2)}) collective-permute-start(f32[8,384]{1,0:T(8,128)S(1)} %get-tuple-element.50.stats_ref), channel_id=1, source_target_pairs={{0,8},{8,0},{4,12},{12,4},{1,9},{9,1},{5,13},{13,5},{2,10},{10,2},... | collective-permute-start | bytes 36872 | tf_op jit(solution)/shard_map/ppermute | solution.py:426
  45.2 4.6 %collective-permute-start.8 = (f32[8,384]{1,0:T(8,128)S(1)}, f32[8,384]{1,0:T(8,128)S(1)}, u32[]{:S(2)}, u32[]{:S(2)}) collective-permute-start(f32[8,384]{1,0:T(8,128)S(1)} %get-tuple-element.45.stats_ref), channel_id=1, source_target_pairs={{0,8},{8,0},{4,12},{12,4},{1,9},{9,1},{5,13},{13,5},{2,10},{10,2},... | collective-permute-start | bytes 36872 | tf_op jit(solution)/shard_map/ppermute | solution.py:426
